TPU v7x, 32 devices: a whole 2x2x4 slice. The times are simulated.
32 devices in a mesh: dp: 4 (over y, core), expert: 2 (over x), group: 4 (over z).
Axes of the slice: x: 2, y: 2, z: 4, core: 2. Of those that a mesh axis runs over, the one named last changes fastest.
Arguments:
- tokens: bfloat16 [256, 7168], P(('dp', 'group')), may hold values from -6 to 6
- expert_ids: int32 [256, 8], P(('dp', 'group')), may hold values from 0 to 255, all different within a row; in each aligned block of 16 rows (0 to 15, 16 to 31, ...) at most 2 rows name the same one
- gate_values: bfloat16 [256, 8], P(('dp', 'group')), may hold values from 0.099609375 to 1
- gate_up: bfloat16 [2, 7168, 2, 2048], P('expert', None, None, 'group'), may hold values from -0.0625 to 0.0625
- down_weight: bfloat16 [2, 2048, 7168], P('expert', 'group'), may hold values from -0.125 to 0.125
- shared_gate_up: bfloat16 [7168, 2, 2048], P('expert', None, 'group'), may hold values from -0.0625 to 0.0625
- shared_down: bfloat16 [2048, 7168], P('group', 'expert'), may hold values from -0.125 to 0.125
Outputs:
- mixed: bfloat16 [256, 7168], P(('dp', 'group'), 'expert')
Inputs may be any that keep to these rules, and one draw needn't show every extreme that they name: `expert_ids`: each row names 8 different routed experts. In each aligned block of 16 rows (the rows of one device) no expert is named by more than 2 rows, and in some blocks one is named by exactly 2 rows.
All inputs are finite; a program needn't handle non-finite values.
Results may differ from a plain program's by a relative error of at most 0.028.
Values may be sent and summed in bfloat16 or wider, within the bound.
No kernel may reach another device: no remote copies, remote signals or barrier semaphores. Data moves between devices by JAX's collectives and lax.ppermute only.
A program may use at most 128 MiB of HBM per device.

v0:
```python
import jax
import jax.numpy as jnp
from jax import lax
from jax.sharding import PartitionSpec as P


def expert_terms(block_tokens, block_weight, gate_up, down_weight):
    model_width = gate_up.shape[1]
    hidden_units = gate_up.shape[3]
    projected = jnp.dot(
        block_tokens,
        gate_up[0].reshape(model_width, 2 * hidden_units),
        preferred_element_type=jnp.float32,
    )
    gate_part = projected[:, :hidden_units]
    up_part = projected[:, hidden_units:]
    hidden = (jax.nn.silu(gate_part) * up_part).astype(jnp.bfloat16)
    product = jnp.dot(hidden, down_weight[0], preferred_element_type=jnp.float32)
    return (product * block_weight.astype(jnp.float32)[:, None]).astype(jnp.bfloat16)


def shared_block(token_columns, shared_gate_up, shared_down):
    column_width = shared_gate_up.shape[0]
    shared_units = shared_gate_up.shape[2]
    shared_partial = jnp.dot(
        token_columns,
        shared_gate_up.reshape(column_width, 2 * shared_units),
        preferred_element_type=jnp.float32,
    )
    shared_pre = lax.psum(shared_partial.astype(jnp.bfloat16), "expert").astype(jnp.float32)
    shared_hidden = (
        jax.nn.silu(shared_pre[:, :shared_units]) * shared_pre[:, shared_units:]
    ).astype(jnp.bfloat16)
    return jnp.dot(shared_hidden, shared_down, preferred_element_type=jnp.float32).astype(
        jnp.bfloat16
    )


def per_device(tokens, expert_ids, gate_values, gate_up, down_weight, shared_gate_up, shared_down):
    slot_index = lax.axis_index("expert")
    column_width = shared_gate_up.shape[0]
    chosen = expert_ids == slot_index
    weight_value = jnp.sum(
        jnp.where(chosen, gate_values.astype(jnp.float32), jnp.float32(0.0)), axis=1
    )
    slot_weight = weight_value.astype(jnp.bfloat16)
    gathered, gathered_weight = (
        lax.all_gather(tokens, "group", axis=0, tiled=True),
        lax.all_gather(slot_weight, "group", axis=0, tiled=True),
    )
    token_columns = lax.dynamic_slice_in_dim(gathered, slot_index * column_width, column_width, 1)
    shared_term = shared_block(token_columns, shared_gate_up, shared_down)
    partial_terms = expert_terms(gathered, gathered_weight, gate_up, down_weight)
    column_total = lax.psum_scatter(
        partial_terms, "expert", scatter_dimension=1, tiled=True
    ).astype(jnp.float32)
    mixed = lax.psum_scatter(
        (column_total + shared_term.astype(jnp.float32)).astype(jnp.bfloat16),
        "group",
        scatter_dimension=0,
        tiled=True,
    )
    return mixed


def solution(mesh):
    in_specs = (
        P(("dp", "group"), None),
        P(("dp", "group"), None),
        P(("dp", "group"), None),
        P("expert", None, None, "group"),
        P("expert", "group", None),
        P("expert", None, "group"),
        P("group", "expert"),
    )
    out_specs = P(("dp", "group"), "expert")
    return jax.shard_map(
        per_device, mesh=mesh, in_specs=in_specs, out_specs=out_specs, check_vma=False
    )
```

profile of v0, /device:TPU:0, one launch (start us, length us, event | category | flops | bytes accessed | tf_op | source)
XLA Modules:
  0.0 119.9 jit_solution(10707480298263581695)
XLA Ops:
  6.5 0.0 all-reduce.3.cloned.1.call-start
  6.5 23.4 %all_gather.6 = bf16[64,7168]{1,0:T(8,128)(2,1)} all-gather(bf16[16,7168]{1,0:T(8,128)(2,1)} %param.7), channel_id=1, replica_groups=mesh['dp'=4,'expert'=2,'group'=4] {'group'}, dimensions={0}, use_global_device_ids=true | all-gather | bytes 1146880 | tf_op jit(solution)/shard_map/all_gather | solution.py:48
  29.9 8.4 %copy.9 = bf16[448,8,2,512]{3,1,2,0:T(8,128)(2,1)} copy(bf16[448,8,2,512]{3,2,1,0:T(2,128)(2,1)} %bitcast.18) | data formatting | bytes 14680064
  38.3 0.0 copy-start.1
  38.3 0.0 copy-start.2
  38.3 0.0 copy-start.3
  38.3 0.0 slice-start
  38.3 5.4 %convolution_convert_fusion.1 = bf16[64,1024]{1,0:T(8,128)(2,1)} fusion(bf16[3584,1024]{1,0:T(8,128)(2,1)} %bitcast.14, bf16[64,7168]{1,0:T(8,128)(2,1)} %all_gather.6, s32[]{:T(128)S(6)} %select_n.8), kind=kOutput, calls=%fused_computation.7 | convolution fusion | flops 469827584 | bytes 7929860 | tf_op jit(solution)/shard_map/dot_general | solution.py:25
  43.7 0.0 all-reduce.3.cloned.1.call-update
  43.8 0.0 reduce-scatter.3.cloned.1.call-start
  43.8 0.0 copy-done.1
  43.8 0.0 copy-done.2
  43.9 0.0 copy-done.3
  43.9 0.6 dynamic-slice
  45.1 0.2 dynamic-update-slice
  45.4 10.1 %all-reduce = bf16[64]{0:T(256)(128)(2,1)S(1)} all-reduce(bf16[64]{0:T(256)(128)(2,1)S(1)} %dynamic-update-slice), channel_id=1, replica_groups=mesh['dp'=4,'expert'=2,'group'=4] {'group'}, use_global_device_ids=true, to_apply=%add | all-reduce | flops 64 | bytes 256
  55.5 0.0 copy-start
  55.5 0.0 slice-start.1
  55.5 10.4 %copy.8 = bf16[896,8,2,512]{3,1,2,0:T(8,128)(2,1)S(1)} copy(bf16[896,8,2,512]{3,2,1,0:T(2,128)(2,1)} %bitcast.17) | data formatting | bytes 29360128
  65.9 0.0 copy-done
  65.9 2.7 %fusion.15 = f32[64,1024]{1,0:T(8,128)S(1)} fusion(bf16[64,7168]{1,0:T(8,128)(2,1)S(1)} %copy-done, bf16[7168,1024]{1,0:T(8,128)(2,1)S(1)} %bitcast.13), kind=kOutput, calls=%fused_computation.19 | convolution fusion | flops 939524096 | bytes 15859712 | tf_op jit(solution)/shard_map/dot_general | solution.py:10
  68.6 0.0 slice-done
  68.6 0.0 slice-done.1
  68.7 2.3 %fusion = bf16[64,7168]{1,0:T(8,128)(2,1)} fusion(bf16[1,512,7168]{2,1,0:T(8,128)(2,1)S(1)} %bitcast.16, f32[64]{0:T(128)S(1)} %convert_element_type.39, f32[64,1024]{1,0:T(8,128)S(1)} %fusion.15), kind=kOutput, calls=%fused_computation.1 | convolution fusion | flops 470876160 | bytes 8519936 | tf_op jit(solution)/shard_map/dot_general | solution.py:18
  71.0 0.0 reduce-scatter.3.cloned.1.call-update
  71.0 0.0 reduce-scatter.5.cloned.1.call-start
  71.0 0.0 all-reduce.3.cloned.1.call-done
  71.1 0.9 convert_element_type.43
  72.0 16.3 %reduce-scatter.3.cloned.1.call-done = bf16[64,3584]{1,0:T(8,128)(2,1)} async-done(((bf16[64,7168]{1,0:T(8,128)(2,1)}), bf16[64,3584]{1,0:T(8,128)(2,1)}) %reduce-scatter.3.cloned.1.call-update) | async-done | bytes 458768 | tf_op jit(solution)/shard_map/reduce_scatter | solution.py:54
  88.3 3.6 %fusion.4 = bf16[64,3584]{1,0:T(8,128)(2,1)} fusion(bf16[512,3584]{1,0:T(8,128)(2,1)} %param.13, bf16[64,3584]{1,0:T(8,128)(2,1)} %reduce-scatter.3.cloned.1.call-done, f32[64,1024]{1,0:T(8,128)S(1)} %convert_element_type.43), kind=kOutput, calls=%fused_computation.6 | convolution fusion | flops 236224512 | bytes 4849664 | tf_op jit(solution)/shard_map/dot_general | solution.py:34
  91.9 0.0 reduce-scatter.5.cloned.1.call-update
  92.0 21.4 %reduce-scatter.5.cloned.1.call-done = bf16[16,3584]{1,0:T(8,128)(2,1)} async-done(((bf16[64,3584]{1,0:T(8,128)(2,1)}), bf16[16,3584]{1,0:T(8,128)(2,1)}) %reduce-scatter.5.cloned.1.call-update) | async-done | bytes 114704 | tf_op jit(solution)/shard_map/reduce_scatter | solution.py:57
  (4 shorter events, 0.0 us)
Async XLA Ops:
  6.5 64.5 %all-reduce.3.cloned.1.call-start = ((), (), s32[]{:S(2)}) async-start(), calls=%async_computation.3 | async-start | bytes 262144 | tf_op jit(solution)/shard_map/psum | solution.py:30
  38.3 5.5 %copy-start.1 = (s32[16,8]{0,1:T(8,128)S(1)}, s32[16,8]{0,1:T(8,128)}, u32[]{:S(2)}) copy-start(s32[16,8]{0,1:T(8,128)} %param.8) | copy-start | bytes 1540
  38.3 5.5 %copy-start.2 = (bf16[16,8]{0,1:T(8,128)(2,1)S(1)}, bf16[16,8]{0,1:T(8,128)(2,1)}, u32[]{:S(2)}) copy-start(bf16[16,8]{0,1:T(8,128)(2,1)} %param.9) | copy-start | bytes 772
  38.3 5.6 %copy-start.3 = (u32[32]{0:T(128)S(1)}, u32[32]{0:T(128)}, u32[]{:S(2)}) copy-start(u32[32]{0:T(128)} %constant.22) | copy-start | bytes 388
  38.3 30.3 %slice-start = ((s8[7340032]{0:T(1024)(128)(4,1)}), s8[3145728]{0:T(1024)(128)(4,1)S(1)}, s32[]{:S(2)}) async-start(s8[7340032]{0:T(1024)(128)(4,1)} %bitcast.15), calls=%async_computation.5 | async-start | bytes 6291456
  43.8 44.5 %reduce-scatter.3.cloned.1.call-start = ((), (), s32[]{:S(2)}) async-start(), calls=%async_computation.2 | async-start | bytes 1376256 | tf_op jit(solution)/shard_map/reduce_scatter | solution.py:54
  55.5 10.4 %copy-start = (bf16[64,7168]{1,0:T(8,128)(2,1)S(1)}, bf16[64,7168]{1,0:T(8,128)(2,1)}, u32[]{:S(2)}) copy-start(bf16[64,7168]{1,0:T(8,128)(2,1)} %all_gather.6) | copy-start | bytes 2752516
  55.5 13.1 %slice-start.1 = ((s8[7340032]{0:T(1024)(128)(4,1)}), s8[4194304]{0:T(1024)(128)(4,1)S(1)}, s32[]{:S(2)}) async-start(s8[7340032]{0:T(1024)(128)(4,1)} %bitcast.15), calls=%async_computation.6 | async-start | bytes 8388608
  71.0 42.4 %reduce-scatter.5.cloned.1.call-start = ((), (), s32[]{:S(2)}) async-start(), calls=%async_computation.4 | async-start | bytes 573440 | tf_op jit(solution)/shard_map/reduce_scatter | solution.py:57
Sparse Core Ops, SparseCore 0:
  43.9 20.9 all-reduce.2
  71.1 17.1 reduce-scatter.2
  92.1 21.2 reduce-scatter.4
where the time goes:
time: 120 us
  waiting for transfers between devices  37.8 us (31%)
  blocking collectives  33.5 us (28%)
  local copies, waits for them, and re-layouts  19.7 us (16%)
  matrix products  14.1 us (12%)
  between operations  13.9 us (12%)
    all_gather x1, blocking collectives, per_device(): lax.all_gather(tokens, 'group', axis=0, tiled=True)  23.4 us
    reduce_scatter x1, waiting for transfers between devices, per_device(): lax.psum_scatter((column_total + shared_term.astype(jnp.float32)).astype(...  21.4 us
    unnamed x17, local copies, waits for them, and re-layouts  19.7 us
    reduce_scatter x1, waiting for transfers between devices, per_device(): lax.psum_scatter(partial_terms, 'expert', scatter_dimension=1, tiled=True)  16.3 us
    unnamed x1, blocking collectives  10.1 us
    dot_general x1, matrix products, shared_block(): jnp.dot(token_columns, shared_gate_up.reshape(column_width, 2 * shared_un...  5.44 us
    dot_general x1, matrix products, shared_block(): jnp.dot(shared_hidden, shared_down, preferred_element_type=jnp.float32)  3.64 us
    dot_general x1, matrix products, expert_terms(): jnp.dot(block_tokens, gate_up[0].reshape(model_width, 2 * hidden_units),...  2.67 us
  transfers between devices with their start and end apart: 3, of which 2 were waited for; matrix products, arithmetic and copies ran while one was open for 14% of the time, Pallas kernels for 0%

commit v1 on v0

v1 whole, which is shorter than its diff:
```python
import jax
import jax.numpy as jnp
from jax import lax
from jax.sharding import PartitionSpec as P

CAP = 2
FORM = "einsum"
GATHER = "permute"
SCATTER = "permute"


def gated(rows, weight):
    model_width, _, units = weight.shape
    if FORM == "interleave":
        zero = jnp.zeros_like(rows)
        lhs = jnp.stack([jnp.stack([rows, zero], 2), jnp.stack([zero, rows], 2)])
        lhs = lhs.reshape(2 * rows.shape[0], 2 * model_width)
        out = jnp.dot(lhs, weight.reshape(2 * model_width, units), preferred_element_type=jnp.float32)
        return out[: rows.shape[0]], out[rows.shape[0]:]
    if FORM == "slice":
        return tuple(jnp.dot(rows, weight[:, i], preferred_element_type=jnp.float32) for i in (0, 1))
    if FORM == "einsum":
        out = jnp.einsum("td,dgf->gtf", rows, weight, preferred_element_type=jnp.float32)
        return out[0], out[1]
    out = jnp.dot(rows, weight.reshape(model_width, 2 * units), preferred_element_type=jnp.float32)
    return out[:, :units], out[:, units:]


def swiglu(gate, up):
    return (jax.nn.silu(gate) * up).astype(jnp.bfloat16)


def gather_blocks(block, axis):
    size = lax.axis_size(axis)
    if GATHER == "ag":
        return lax.all_gather(block, axis)
    if GATHER == "a2a":
        return lax.all_to_all(jnp.broadcast_to(block[None], (size,) + block.shape), axis, 0, 0)
    pieces = [block]
    for step in range(1, size):
        pieces.append(lax.ppermute(block, axis, [(i, (i - step) % size) for i in range(size)]))
    return jnp.stack(pieces)


def exchange(blocks, axis):
    size = lax.axis_size(axis)
    arrived = [blocks[0]]
    for step in range(1, size):
        arrived.append(lax.ppermute(blocks[step], axis, [(i, (i + step) % size) for i in range(size)]))
    return arrived


def per_device(tokens, expert_ids, gate_values, gate_up, down_weight, shared_gate_up, shared_down):
    experts, groups = lax.axis_size("expert"), lax.axis_size("group")
    me = lax.axis_index("expert")
    count, width = tokens.shape
    columns = shared_gate_up.shape[0]
    units = shared_gate_up.shape[2]

    slots = jnp.arange(experts, dtype=jnp.int32)
    named = expert_ids[None] == slots[:, None, None]
    chosen = jnp.any(named, axis=2)
    weight = jnp.sum(jnp.where(named, gate_values.astype(jnp.float32)[None], 0.0), axis=2)
    rank = jnp.sum(
        jnp.where(jnp.tril(jnp.ones((count, count), jnp.bool_), -1)[None], chosen[:, None, :], False).astype(jnp.int32),
        axis=2,
    )
    places = jnp.arange(CAP, dtype=jnp.int32)[None, :, None]
    selection = (chosen[:, None, :] & (rank[:, None, :] == places))
    mine = lax.dynamic_index_in_dim(selection, me, 0, keepdims=False).astype(jnp.bfloat16)
    rows = jnp.dot(mine, tokens, preferred_element_type=jnp.float32).astype(jnp.bfloat16)

    own_columns = lax.dynamic_slice_in_dim(tokens, me * columns, columns, 1)
    all_rows = gather_blocks(rows, "group").reshape(groups * CAP, width)
    all_columns = gather_blocks(own_columns, "group").reshape(groups * count, columns)

    shared_gate, shared_up = gated(all_columns, shared_gate_up)
    partial = jnp.concatenate([shared_gate, shared_up], 1)
    if experts == 2:
        other = lax.ppermute(partial.astype(jnp.bfloat16), "expert", [(0, 1), (1, 0)])
        pre = partial + other.astype(jnp.float32)
    else:
        pre = lax.psum(partial.astype(jnp.bfloat16), "expert").astype(jnp.float32)

    hidden = swiglu(*gated(all_rows, gate_up[0]))
    product = jnp.dot(hidden, down_weight[0], preferred_element_type=jnp.float32).astype(jnp.bfloat16)
    product = product.reshape(groups * CAP, experts, columns)
    if experts == 2:
        keep = lax.dynamic_index_in_dim(product, me, 1, keepdims=False)
        away = lax.dynamic_index_in_dim(product, 1 - me, 1, keepdims=False)
        came = lax.ppermute(away, "expert", [(0, 1), (1, 0)])
        first = jnp.where(me == 0, keep, came)
        second = jnp.where(me == 0, came, keep)
        routed = jnp.stack([first, second]).reshape(experts, groups, CAP, columns)
    else:
        routed = lax.all_to_all(product, "expert", 1, 0).reshape(experts, groups, CAP, columns)

    shared_hidden = swiglu(pre[:, :units], pre[:, units:])
    shared = jnp.dot(shared_hidden, shared_down, preferred_element_type=jnp.float32).astype(jnp.bfloat16)

    arrived = exchange(shared.reshape(groups, count, columns), "group")
    routed_arrived = exchange(jnp.swapaxes(routed, 0, 1).reshape(groups, experts * CAP, columns), "group")
    total = sum(a.astype(jnp.float32) for a in arrived)
    terms = sum(a.astype(jnp.float32) for a in routed_arrived)
    spread = jnp.where(selection, weight[:, None, :], 0.0).reshape(experts * CAP, count)
    for j in range(experts * CAP):
        total = total + spread[j][:, None] * terms[j][None, :]
    return total.astype(jnp.bfloat16)


def solution(mesh):
    in_specs = (
        P(("dp", "group"), None),
        P(("dp", "group"), None),
        P(("dp", "group"), None),
        P("expert", None, None, "group"),
        P("expert", "group", None),
        P("expert", None, "group"),
        P("group", "expert"),
    )
    out_specs = P(("dp", "group"), "expert")
    return jax.shard_map(
        per_device, mesh=mesh, in_specs=in_specs, out_specs=out_specs, check_vma=False
    )
```

time: 120 us -> 55.1 us (0.46)
  blocking collectives: 33.5 us -> 0 us
  waiting for transfers between devices: 37.8 us -> 10.9 us
  starting transfers between devices: 0.09 us -> 22.3 us
  local copies, waits for them, and re-layouts: 19.7 us -> 2.51 us
  between operations: 13.9 us -> 0.23 us
  other arithmetic: 0.95 us -> 5.07 us
    reduce_scatter x2 -> x0, waiting for transfers between devices: 37.7 us -> none  [the longest x1 21.4 us: per_device(): lax.psum_scatter((column_total + shared_term.astype(jnp.float32)).astype(...]
    all_gather x1 -> x0, blocking collectives: 23.4 us -> none  [per_device(): lax.all_gather(tokens, 'group', axis=0, tiled=True)]
    ppermute x0 -> x14, starting transfers between devices: none -> 22.3 us  [the longest x6 10.1 us: gather_blocks(): lax.ppermute(block, axis, [(i, (i - step) % size) for i in range(size)])]
    unnamed x17 -> x8, local copies, waits for them, and re-layouts: 19.7 us -> 0.02 us
    ppermute x0 -> x14, waiting for transfers between devices: none -> 10.9 us  [the longest x6 4.75 us: exchange(): lax.ppermute(blocks[step], axis, [(i, (i + step) % size) for i in range(s...]
    unnamed x1 -> x0, blocking collectives: 10.1 us -> none
    another operation x0 -> x2, other arithmetic: none -> 1.55 us  [gather_blocks(): return jnp.stack(pieces)]
    dot_general x4 -> x5, matrix products: 14.1 us -> 13.9 us  [the longest x2 12 us: gated(): jnp.einsum('td,dgf->gtf', rows, weight, preferred_element_type=jnp.float32)]
  transfers between devices with their start and end apart: 3 -> 14, of which waited for: 2 -> 4; matrix products, arithmetic and copies ran while one was open for 14% -> 34% of each run, Pallas kernels for 0% -> 0%
where the time goes in v1:
time: 55.1 us; the launch traced here: 54.9 us
  starting transfers between devices  22.3 us (40%)
  matrix products  13.9 us (25%)
  waiting for transfers between devices  10.9 us (20%)
  other arithmetic  5.07 us (9%)
  local copies, waits for them, and re-layouts  2.51 us (5%)
    dot_general x2, matrix products, gated(): jnp.einsum('td,dgf->gtf', rows, weight, preferred_element_type=jnp.float32)  12 us
    ppermute x6, starting transfers between devices, gather_blocks(): lax.ppermute(block, axis, [(i, (i - step) % size) for i in range(size)])  10.1 us
    ppermute x6, starting transfers between devices, exchange(): lax.ppermute(blocks[step], axis, [(i, (i + step) % size) for i in range(s...  9.1 us
    ppermute x6, waiting for transfers between devices, exchange(): lax.ppermute(blocks[step], axis, [(i, (i + step) % size) for i in range(s...  4.75 us
    ppermute x1, waiting for transfers between devices, per_device(): lax.ppermute(partial.astype(jnp.bfloat16), 'expert', [(0, 1), (1, 0)])  3.43 us
    ppermute x1, waiting for transfers between devices, per_device(): came = lax.ppermute(away, 'expert', [(0, 1), (1, 0)])  2.68 us
    ppermute x1, starting transfers between devices, per_device(): lax.ppermute(partial.astype(jnp.bfloat16), 'expert', [(0, 1), (1, 0)])  1.56 us
    another operation x2, other arithmetic, gather_blocks(): return jnp.stack(pieces)  1.55 us
  transfers between devices with their start and end apart: 14, of which 4 were waited for; matrix products, arithmetic and copies ran while one was open for 34% of the time, Pallas kernels for 0%

profile of v1, /device:TPU:0, one launch (start us, length us, event | category | flops | bytes accessed | tf_op | source)
XLA Modules:
  0.0 54.9 jit_solution(11394468085402270182)
XLA Ops:
  0.0 0.7 %fusion.18 = pred[2,16]{1,0:T(4,128)(4,1)S(1)} fusion(s32[16,8]{0,1:T(8,128)} %param.8), kind=kLoop, calls=%fused_computation.38 | loop fusion | flops 480 | bytes 544 | tf_op jit(solution)/shard_map/reduce_or | solution.py:62
  0.8 0.1 iota_compare_fusion
  0.8 0.1 convert_reduce_fusion
  1.0 0.2 convolution_convert_fusion.1
  1.2 5.1 %collective-permute-start.7 = (bf16[2,7168]{1,0:T(2,128)(2,1)S(1)}, bf16[2,7168]{1,0:T(2,128)(2,1)S(1)}, u32[]{:S(2)}, u32[]{:S(2)}) collective-permute-start(bf16[2,7168]{1,0:T(2,128)(2,1)S(1)} %convolution_convert_fusion.1), channel_id=1, source_target_pairs={{0,3},{1,0},{2,1},{3,2},{4,7},{5,4},{6,5},{7,6},{8,11},{9,8},{10,9... | collective-permute-start | bytes 86024 | tf_op jit(solution)/shard_map/ppermute | solution.py:41
  6.3 0.0 collective-permute-start.8
  6.3 1.0 %collective-permute-start.9 = (bf16[2,7168]{1,0:T(2,128)(2,1)S(1)}, bf16[2,7168]{1,0:T(2,128)(2,1)S(1)}, u32[]{:S(2)}, u32[]{:S(2)}) collective-permute-start(bf16[2,7168]{1,0:T(2,128)(2,1)S(1)} %convolution_convert_fusion.1), channel_id=1, source_target_pairs={{0,1},{1,2},{2,3},{3,0},{4,5},{5,6},{6,7},{7,4},{8,9},{9,10},{10,1... | collective-permute-start | bytes 86024 | tf_op jit(solution)/shard_map/ppermute | solution.py:41
  7.3 0.7 %constant_dynamic-slice_fusion.2 = bf16[16,3584]{1,0:T(8,128)(2,1)} fusion(bf16[16,7168]{1,0:T(8,128)(2,1)S(1)} %copy-done, s32[]{:T(128)S(6)} %select_n.39), kind=kLoop, calls=%fused_computation.45 | loop fusion | bytes 229380 | tf_op jit(solution)/shard_map/dynamic_slice | solution.py:73
  8.0 2.8 %collective-permute-start = (bf16[16,3584]{1,0:T(8,128)(2,1)}, bf16[16,3584]{1,0:T(8,128)(2,1)}, u32[]{:S(2)}, u32[]{:S(2)}) collective-permute-start(bf16[16,3584]{1,0:T(8,128)(2,1)} %constant_dynamic-slice_fusion.2), channel_id=1, source_target_pairs={{0,3},{1,0},{2,1},{3,2},{4,7},{5,4},{6,5},{7,6},{8,11},{9,8},{10,9... | collective-permute-start | bytes 344072 | tf_op jit(solution)/shard_map/ppermute | solution.py:41
  10.8 1.1 %collective-permute-start.1 = (bf16[16,3584]{1,0:T(8,128)(2,1)}, bf16[16,3584]{1,0:T(8,128)(2,1)}, u32[]{:S(2)}, u32[]{:S(2)}) collective-permute-start(bf16[16,3584]{1,0:T(8,128)(2,1)} %constant_dynamic-slice_fusion.2), channel_id=1, source_target_pairs={{0,2},{1,3},{2,0},{3,1},{4,6},{5,7},{6,4},{7,5},{8,10},{9,11},{10,... | collective-permute-start | bytes 344072 | tf_op jit(solution)/shard_map/ppermute | solution.py:41
  11.9 0.6 %fusion.33 = bf16[1,16,3584]{2,1,0:T(8,128)(2,1)} fusion(bf16[16,7168]{1,0:T(8,128)(2,1)S(1)} %copy-done, s32[]{:T(128)S(6)} %select_n.39), kind=kLoop, calls=%fused_computation.58 | loop fusion | bytes 229380 | tf_op jit(solution)/shard_map/stack | solution.py:42
  12.6 0.7 %convert_element_type.70 = f32[16,8]{0,1:T(8,128)S(1)} convert(bf16[16,8]{0,1:T(8,128)(2,1)} %param.9) | non-fusion elementwise | flops 128 | bytes 768 | tf_op jit(solution)/shard_map/convert_element_type | solution.py:63
  13.2 0.7 %select_reduce_fusion = f32[2,16]{1,0:T(2,128)S(1)} fusion(f32[16,8]{0,1:T(8,128)S(1)} %convert_element_type.70, s32[16,8]{0,1:T(8,128)} %param.8), kind=kLoop, calls=%fused_computation.35 | loop fusion | flops 736 | bytes 1152 | tf_op jit(solution)/shard_map/reduce_sum | solution.py:63
  14.0 0.1 eq.47
  14.0 0.1 and_select_fusion
  14.1 0.0 collective-permute-start.2
  14.1 0.0 collective-permute-done.9
  14.2 0.2 pad_maximum_fusion.2
  14.4 0.0 slice-start
  14.4 0.7 %reshape.67 = bf16[8,7168,1]{1,0,2:T(8,128)(2,1)} reshape(bf16[4,2,7168]{2,1,0:T(2,128)(2,1)S(1)} %pad_maximum_fusion.2) | data formatting | bytes 229376 | tf_op jit(solution)/shard_map/reshape | solution.py:74
  15.1 7.5 %fusion.8 = f32[2,8,512]{2,1,0:T(8,128)S(1)} fusion(bf16[8,7168,1]{1,0,2:T(8,128)(2,1)} %reshape.67, bf16[7168,2,512]{2,1,0:T(2,128)(2,1)} %bitcast.60), kind=kOutput, calls=%fused_computation.9 | convolution fusion | flops 117440512 | bytes 14827520 | tf_op jit(solution)/shard_map/td,dgf->gtf/dot_general | solution.py:23
  22.6 1.1 %convolution_convert_fusion = bf16[8,7168]{1,0:T(8,128)(2,1)S(1)} fusion(bf16[1,512,7168]{2,1,0:T(8,128)(2,1)S(1)} %bitcast.62, f32[2,8,512]{2,1,0:T(8,128)S(1)} %fusion.8), kind=kOutput, calls=%fused_computation.2 | convolution fusion | flops 58802176 | bytes 7487488 | tf_op jit(solution)/shard_map/dot_general | solution.py:86
  23.6 1.5 %collective-permute-start.10 = (bf16[8,3584]{1,0:T(8,128)(2,1)S(1)}, bf16[8,3584]{1,0:T(8,128)(2,1)S(1)}, u32[]{:S(2)}, u32[]{:S(2)}) collective-permute-start(bf16[8,3584]{1,0:T(8,128)(2,1)S(1)} %dynamic-slice_bitcast_fusion), channel_id=1, source_target_pairs={{0,4},{4,0},{1,5},{5,1},{2,6},{6,2},{3,7},{7,3},{8,12},{12,8},{9,1... | collective-permute-start | bytes 172040 | tf_op jit(solution)/shard_map/ppermute | solution.py:91
  25.2 2.7 %collective-permute-done.10 = bf16[8,3584]{1,0:T(8,128)(2,1)S(1)} collective-permute-done((bf16[8,3584]{1,0:T(8,128)(2,1)S(1)}, bf16[8,3584]{1,0:T(8,128)(2,1)S(1)}, u32[]{:S(2)}, u32[]{:S(2)}) %collective-permute-start.10) | collective-permute-done | bytes 57376 | tf_op jit(solution)/shard_map/ppermute | solution.py:91
  27.9 0.2 maximum_bitcast_fusion
  28.1 0.1 fusion.28
  28.2 2.4 %collective-permute-start.11 = (bf16[4,3584]{1,0:T(4,128)(2,1)S(1)}, bf16[4,3584]{1,0:T(4,128)(2,1)S(1)}, u32[]{:S(2)}, u32[]{:S(2)}) collective-permute-start(bf16[4,3584]{1,0:T(4,128)(2,1)S(1)} %squeeze.46), channel_id=1, source_target_pairs={{0,1},{1,2},{2,3},{3,0},{4,5},{5,6},{6,7},{7,4},{8,9},{9,10},{10,1... | collective-permute-start | bytes 86024 | tf_op jit(solution)/shard_map/ppermute | solution.py:49
  30.6 2.1 %collective-permute-start.12 = (bf16[4,3584]{1,0:T(4,128)(2,1)S(1)}, bf16[4,3584]{1,0:T(4,128)(2,1)S(1)}, u32[]{:S(2)}, u32[]{:S(2)}) collective-permute-start(bf16[4,3584]{1,0:T(4,128)(2,1)S(1)} %squeeze.47), channel_id=1, source_target_pairs={{0,2},{1,3},{2,0},{3,1},{4,6},{5,7},{6,4},{7,5},{8,10},{9,11},{10,... | collective-permute-start | bytes 86024 | tf_op jit(solution)/shard_map/ppermute | solution.py:49
  32.7 0.1 reshape.65
  32.8 0.0 copy-start.1
  32.8 0.0 collective-permute-done
  32.8 0.4 collective-permute-start.13
  33.2 0.0 collective-permute-done.1
  33.2 1.3 %pad_maximum_fusion = bf16[4,16,3584]{2,1,0:T(8,128)(2,1)S(1)} fusion(bf16[1,16,3584]{2,1,0:T(8,128)(2,1)} %bitcast.3, bf16[1,16,3584]{2,1,0:T(8,128)(2,1)} %bitcast.2, bf16[1,16,3584]{2,1,0:T(8,128)(2,1)} %bitcast.1, bf16[1,16,3584]{2,1,0:T(8,128)(2,1)} %fusion.33), kind=kLoop, calls=%fused_computation.10 | loop fusion | flops 688128 | bytes 917504 | tf_op jit(solution)/shard_map/stack | solution.py:42
  34.6 4.5 %fusion.5 = f32[2,64,512]{2,1,0:T(8,128)S(1)} fusion(bf16[64,3584,1]{1,0,2:T(8,128)(2,1)S(1)} %bitcast.65, bf16[3584,2,512]{2,1,0:T(2,128)(2,1)} %param.12), kind=kOutput, calls=%fused_computation.8 | convolution fusion | flops 469762048 | bytes 8060928 | tf_op jit(solution)/shard_map/td,dgf->gtf/dot_general | solution.py:23
  39.1 1.6 %collective-permute-start.3 = (bf16[64,1024]{1,0:T(8,128)(2,1)S(1)}, bf16[64,1024]{1,0:T(8,128)(2,1)S(1)}, u32[]{:S(2)}, u32[]{:S(2)}) collective-permute-start(bf16[64,1024]{1,0:T(8,128)(2,1)S(1)} %fusion.11), channel_id=1, source_target_pairs={{0,4},{4,0},{1,5},{5,1},{2,6},{6,2},{3,7},{7,3},{8,12},{12,8},{9,1... | collective-permute-start | bytes 393224 | tf_op jit(solution)/shard_map/ppermute | solution.py:80
  40.7 0.0 collective-permute-done.11
  40.7 0.0 collective-permute-done.12
  40.7 0.0 collective-permute-done.13
  40.7 3.4 %collective-permute-done.3 = bf16[64,1024]{1,0:T(8,128)(2,1)S(1)} collective-permute-done((bf16[64,1024]{1,0:T(8,128)(2,1)S(1)}, bf16[64,1024]{1,0:T(8,128)(2,1)S(1)}, u32[]{:S(2)}, u32[]{:S(2)}) %collective-permute-start.3) | collective-permute-done | bytes 131104 | tf_op jit(solution)/shard_map/ppermute | solution.py:80
  44.2 0.7 %convolution_convert_fusion.2 = bf16[64,3584]{1,0:T(8,128)(2,1)S(1)} fusion(bf16[512,3584]{1,0:T(8,128)(2,1)S(1)} %copy-done.1, f32[64,1024]{1,0:T(8,128)S(1)} %convert_add_fusion), kind=kOutput, calls=%fused_computation.7 | convolution fusion | flops 235307008 | bytes 4390912 | tf_op jit(solution)/shard_map/dot_general | solution.py:99
  45.0 1.5 %collective-permute-start.4 = (bf16[16,3584]{1,0:T(8,128)(2,1)S(1)}, bf16[16,3584]{1,0:T(8,128)(2,1)S(1)}, u32[]{:S(2)}, u32[]{:S(2)}) collective-permute-start(bf16[16,3584]{1,0:T(8,128)(2,1)S(1)} %get-tuple-element.9), channel_id=1, source_target_pairs={{0,1},{1,2},{2,3},{3,0},{4,5},{5,6},{6,7},{7,4},{8,9},{9,10},{10,1... | collective-permute-start | bytes 344072 | tf_op jit(solution)/shard_map/ppermute | solution.py:49
  46.5 0.9 %collective-permute-start.5 = (bf16[16,3584]{1,0:T(8,128)(2,1)S(1)}, bf16[16,3584]{1,0:T(8,128)(2,1)S(1)}, u32[]{:S(2)}, u32[]{:S(2)}) collective-permute-start(bf16[16,3584]{1,0:T(8,128)(2,1)S(1)} %get-tuple-element.11), channel_id=1, source_target_pairs={{0,2},{1,3},{2,0},{3,1},{4,6},{5,7},{6,4},{7,5},{8,10},{9,11},{10,... | collective-permute-start | bytes 344072 | tf_op jit(solution)/shard_map/ppermute | solution.py:49
  47.4 1.8 %collective-permute-start.6 = (bf16[16,3584]{1,0:T(8,128)(2,1)S(1)}, bf16[16,3584]{1,0:T(8,128)(2,1)S(1)}, u32[]{:S(2)}, u32[]{:S(2)}) collective-permute-start(bf16[16,3584]{1,0:T(8,128)(2,1)S(1)} %get-tuple-element.10), channel_id=1, source_target_pairs={{0,3},{1,0},{2,1},{3,2},{4,7},{5,4},{6,5},{7,6},{8,11},{9,8},{10,9... | collective-permute-start | bytes 344072 | tf_op jit(solution)/shard_map/ppermute | solution.py:49
  49.2 0.1 slice_reduce_fusion.3
  49.3 2.4 %collective-permute-done.4 = bf16[16,3584]{1,0:T(8,128)(2,1)S(1)} collective-permute-done((bf16[16,3584]{1,0:T(8,128)(2,1)S(1)}, bf16[16,3584]{1,0:T(8,128)(2,1)S(1)}, u32[]{:S(2)}, u32[]{:S(2)}) %collective-permute-start.4) | collective-permute-done | bytes 114720 | tf_op jit(solution)/shard_map/ppermute | solution.py:49
  51.8 2.3 %collective-permute-done.5 = bf16[16,3584]{1,0:T(8,128)(2,1)S(1)} collective-permute-done((bf16[16,3584]{1,0:T(8,128)(2,1)S(1)}, bf16[16,3584]{1,0:T(8,128)(2,1)S(1)}, u32[]{:S(2)}, u32[]{:S(2)}) %collective-permute-start.5) | collective-permute-done | bytes 114720 | tf_op jit(solution)/shard_map/ppermute | solution.py:49
  54.1 0.8 %add_convert_fusion = bf16[16,3584]{1,0:T(8,128)(2,1)} fusion(bf16[16,3584]{1,0:T(8,128)(2,1)S(1)} %collective-permute-done.6, bf16[16,3584]{1,0:T(8,128)(2,1)S(1)} %collective-permute-done.5, bf16[16,3584]{1,0:T(8,128)(2,1)S(1)} %collective-permute-done.4, bf16[64,3584]{1,0:T(8,128)(2,1)S(1)} %convolution_convert_fusion.2, f32[3584]{0:T(1024)S(1)} %get-tuple-element.6, ...), kind=kLoop, calls=%fused_computation.13 | loop fusion | flops 917504 | bytes 631040 | tf_op jit(solution)/shard_map/convert_element_type | solution.py:108
  (32 shorter events, 0.3 us)
Async XLA Ops:
  0.0 1.0 %copy-start = (bf16[16,7168]{1,0:T(8,128)(2,1)S(1)}, bf16[16,7168]{1,0:T(8,128)(2,1)}, u32[]{:S(2)}) copy-start(bf16[16,7168]{1,0:T(8,128)(2,1)} %param.7) | copy-start | bytes 688132
  1.2 13.0 %collective-permute-start.7 = (bf16[2,7168]{1,0:T(2,128)(2,1)S(1)}, bf16[2,7168]{1,0:T(2,128)(2,1)S(1)}, u32[]{:S(2)}, u32[]{:S(2)}) collective-permute-start(bf16[2,7168]{1,0:T(2,128)(2,1)S(1)} %convolution_convert_fusion.1), channel_id=1, source_target_pairs={{0,3},{1,0},{2,1},{3,2},{4,7},{5,4},{6,5},{7,6},{8,11},{9,8},{10,9... | collective-permute-start | bytes 86024 | tf_op jit(solution)/shard_map/ppermute | solution.py:41
  6.3 7.8 %collective-permute-start.8 = (bf16[2,7168]{1,0:T(2,128)(2,1)S(1)}, bf16[2,7168]{1,0:T(2,128)(2,1)S(1)}, u32[]{:S(2)}, u32[]{:S(2)}) collective-permute-start(bf16[2,7168]{1,0:T(2,128)(2,1)S(1)} %convolution_convert_fusion.1), channel_id=1, source_target_pairs={{0,2},{1,3},{2,0},{3,1},{4,6},{5,7},{6,4},{7,5},{8,10},{9,11},{10,... | collective-permute-start | bytes 86024 | tf_op jit(solution)/shard_map/ppermute | solution.py:41
  6.3 7.9 %collective-permute-start.9 = (bf16[2,7168]{1,0:T(2,128)(2,1)S(1)}, bf16[2,7168]{1,0:T(2,128)(2,1)S(1)}, u32[]{:S(2)}, u32[]{:S(2)}) collective-permute-start(bf16[2,7168]{1,0:T(2,128)(2,1)S(1)} %convolution_convert_fusion.1), channel_id=1, source_target_pairs={{0,1},{1,2},{2,3},{3,0},{4,5},{5,6},{6,7},{7,4},{8,9},{9,10},{10,1... | collective-permute-start | bytes 86024 | tf_op jit(solution)/shard_map/ppermute | solution.py:41
  8.0 24.9 %collective-permute-start = (bf16[16,3584]{1,0:T(8,128)(2,1)}, bf16[16,3584]{1,0:T(8,128)(2,1)}, u32[]{:S(2)}, u32[]{:S(2)}) collective-permute-start(bf16[16,3584]{1,0:T(8,128)(2,1)} %constant_dynamic-slice_fusion.2), channel_id=1, source_target_pairs={{0,3},{1,0},{2,1},{3,2},{4,7},{5,4},{6,5},{7,6},{8,11},{9,8},{10,9... | collective-permute-start | bytes 344072 | tf_op jit(solution)/shard_map/ppermute | solution.py:41
  10.8 22.5 %collective-permute-start.1 = (bf16[16,3584]{1,0:T(8,128)(2,1)}, bf16[16,3584]{1,0:T(8,128)(2,1)}, u32[]{:S(2)}, u32[]{:S(2)}) collective-permute-start(bf16[16,3584]{1,0:T(8,128)(2,1)} %constant_dynamic-slice_fusion.2), channel_id=1, source_target_pairs={{0,2},{1,3},{2,0},{3,1},{4,6},{5,7},{6,4},{7,5},{8,10},{9,11},{10,... | collective-permute-start | bytes 344072 | tf_op jit(solution)/shard_map/ppermute | solution.py:41
  14.1 19.1 %collective-permute-start.2 = (bf16[16,3584]{1,0:T(8,128)(2,1)}, bf16[16,3584]{1,0:T(8,128)(2,1)}, u32[]{:S(2)}, u32[]{:S(2)}) collective-permute-start(bf16[16,3584]{1,0:T(8,128)(2,1)} %constant_dynamic-slice_fusion.2), channel_id=1, source_target_pairs={{0,1},{1,2},{2,3},{3,0},{4,5},{5,6},{6,7},{7,4},{8,9},{9,10},{10,1... | collective-permute-start | bytes 344072 | tf_op jit(solution)/shard_map/ppermute | solution.py:41
  14.4 8.2 %slice-start = ((s8[7340032]{0:T(1024)(128)(4,1)}), s8[3145728]{0:T(1024)(128)(4,1)S(1)}, s32[]{:S(2)}) async-start(s8[7340032]{0:T(1024)(128)(4,1)} %bitcast.61), calls=%async_computation | async-start | bytes 6291456
  15.1 7.5 %slice-start.1 = ((s8[7340032]{0:T(1024)(128)(4,1)}), s8[4194304]{0:T(1024)(128)(4,1)S(1)}, s32[]{:S(2)}) async-start(s8[7340032]{0:T(1024)(128)(4,1)} %bitcast.61), calls=%async_computation.1 | async-start | bytes 8388608
  23.6 4.2 %collective-permute-start.10 = (bf16[8,3584]{1,0:T(8,128)(2,1)S(1)}, bf16[8,3584]{1,0:T(8,128)(2,1)S(1)}, u32[]{:S(2)}, u32[]{:S(2)}) collective-permute-start(bf16[8,3584]{1,0:T(8,128)(2,1)S(1)} %dynamic-slice_bitcast_fusion), channel_id=1, source_target_pairs={{0,4},{4,0},{1,5},{5,1},{2,6},{6,2},{3,7},{7,3},{8,12},{12,8},{9,1... | collective-permute-start | bytes 172040 | tf_op jit(solution)/shard_map/ppermute | solution.py:91
  28.2 12.5 %collective-permute-start.11 = (bf16[4,3584]{1,0:T(4,128)(2,1)S(1)}, bf16[4,3584]{1,0:T(4,128)(2,1)S(1)}, u32[]{:S(2)}, u32[]{:S(2)}) collective-permute-start(bf16[4,3584]{1,0:T(4,128)(2,1)S(1)} %squeeze.46), channel_id=1, source_target_pairs={{0,1},{1,2},{2,3},{3,0},{4,5},{5,6},{6,7},{7,4},{8,9},{9,10},{10,1... | collective-permute-start | bytes 86024 | tf_op jit(solution)/shard_map/ppermute | solution.py:49
  30.6 10.1 %collective-permute-start.12 = (bf16[4,3584]{1,0:T(4,128)(2,1)S(1)}, bf16[4,3584]{1,0:T(4,128)(2,1)S(1)}, u32[]{:S(2)}, u32[]{:S(2)}) collective-permute-start(bf16[4,3584]{1,0:T(4,128)(2,1)S(1)} %squeeze.47), channel_id=1, source_target_pairs={{0,2},{1,3},{2,0},{3,1},{4,6},{5,7},{6,4},{7,5},{8,10},{9,11},{10,... | collective-permute-start | bytes 86024 | tf_op jit(solution)/shard_map/ppermute | solution.py:49
  32.8 11.4 %copy-start.1 = (bf16[512,3584]{1,0:T(8,128)(2,1)S(1)}, bf16[512,3584]{1,0:T(8,128)(2,1)}, u32[]{:S(2)}) copy-start(bf16[512,3584]{1,0:T(8,128)(2,1)} %param.13) | copy-start | bytes 11010052
  32.8 7.9 %collective-permute-start.13 = (bf16[4,3584]{1,0:T(4,128)(2,1)S(1)}, bf16[4,3584]{1,0:T(4,128)(2,1)S(1)}, u32[]{:S(2)}, u32[]{:S(2)}) collective-permute-start(bf16[4,3584]{1,0:T(4,128)(2,1)S(1)} %squeeze.48), channel_id=1, source_target_pairs={{0,3},{1,0},{2,1},{3,2},{4,7},{5,4},{6,5},{7,6},{8,11},{9,8},{10,9... | collective-permute-start | bytes 86024 | tf_op jit(solution)/shard_map/ppermute | solution.py:49
  39.1 5.0 %collective-permute-start.3 = (bf16[64,1024]{1,0:T(8,128)(2,1)S(1)}, bf16[64,1024]{1,0:T(8,128)(2,1)S(1)}, u32[]{:S(2)}, u32[]{:S(2)}) collective-permute-start(bf16[64,1024]{1,0:T(8,128)(2,1)S(1)} %fusion.11), channel_id=1, source_target_pairs={{0,4},{4,0},{1,5},{5,1},{2,6},{6,2},{3,7},{7,3},{8,12},{12,8},{9,1... | collective-permute-start | bytes 393224 | tf_op jit(solution)/shard_map/ppermute | solution.py:80
  45.0 6.8 %collective-permute-start.4 = (bf16[16,3584]{1,0:T(8,128)(2,1)S(1)}, bf16[16,3584]{1,0:T(8,128)(2,1)S(1)}, u32[]{:S(2)}, u32[]{:S(2)}) collective-permute-start(bf16[16,3584]{1,0:T(8,128)(2,1)S(1)} %get-tuple-element.9), channel_id=1, source_target_pairs={{0,1},{1,2},{2,3},{3,0},{4,5},{5,6},{6,7},{7,4},{8,9},{9,10},{10,1... | collective-permute-start | bytes 344072 | tf_op jit(solution)/shard_map/ppermute | solution.py:49
  46.5 7.6 %collective-permute-start.5 = (bf16[16,3584]{1,0:T(8,128)(2,1)S(1)}, bf16[16,3584]{1,0:T(8,128)(2,1)S(1)}, u32[]{:S(2)}, u32[]{:S(2)}) collective-permute-start(bf16[16,3584]{1,0:T(8,128)(2,1)S(1)} %get-tuple-element.11), channel_id=1, source_target_pairs={{0,2},{1,3},{2,0},{3,1},{4,6},{5,7},{6,4},{7,5},{8,10},{9,11},{10,... | collective-permute-start | bytes 344072 | tf_op jit(solution)/shard_map/ppermute | solution.py:49
  47.4 6.7 %collective-permute-start.6 = (bf16[16,3584]{1,0:T(8,128)(2,1)S(1)}, bf16[16,3584]{1,0:T(8,128)(2,1)S(1)}, u32[]{:S(2)}, u32[]{:S(2)}) collective-permute-start(bf16[16,3584]{1,0:T(8,128)(2,1)S(1)} %get-tuple-element.10), channel_id=1, source_target_pairs={{0,3},{1,0},{2,1},{3,2},{4,7},{5,4},{6,5},{7,6},{8,11},{9,8},{10,9... | collective-permute-start | bytes 344072 | tf_op jit(solution)/shard_map/ppermute | solution.py:49

commit v2 on v1

--- a/solution.py
+++ b/solution.py
@@ -3,27 +3,13 @@
 from jax import lax
 from jax.sharding import PartitionSpec as P
 
+
 CAP = 2
-FORM = "einsum"
-GATHER = "permute"
-SCATTER = "permute"
 
 
 def gated(rows, weight):
-    model_width, _, units = weight.shape
-    if FORM == "interleave":
-        zero = jnp.zeros_like(rows)
-        lhs = jnp.stack([jnp.stack([rows, zero], 2), jnp.stack([zero, rows], 2)])
-        lhs = lhs.reshape(2 * rows.shape[0], 2 * model_width)
-        out = jnp.dot(lhs, weight.reshape(2 * model_width, units), preferred_element_type=jnp.float32)
-        return out[: rows.shape[0]], out[rows.shape[0]:]
-    if FORM == "slice":
-        return tuple(jnp.dot(rows, weight[:, i], preferred_element_type=jnp.float32) for i in (0, 1))
-    if FORM == "einsum":
-        out = jnp.einsum("td,dgf->gtf", rows, weight, preferred_element_type=jnp.float32)
-        return out[0], out[1]
-    out = jnp.dot(rows, weight.reshape(model_width, 2 * units), preferred_element_type=jnp.float32)
-    return out[:, :units], out[:, units:]
+    out = jnp.einsum("td,dgf->gtf", rows, weight, preferred_element_type=jnp.float32)
+    return out[0], out[1]
 
 
 def swiglu(gate, up):
@@ -32,14 +18,10 @@
 
 def gather_blocks(block, axis):
     size = lax.axis_size(axis)
-    if GATHER == "ag":
-        return lax.all_gather(block, axis)
-    if GATHER == "a2a":
-        return lax.all_to_all(jnp.broadcast_to(block[None], (size,) + block.shape), axis, 0, 0)
     pieces = [block]
     for step in range(1, size):
         pieces.append(lax.ppermute(block, axis, [(i, (i - step) % size) for i in range(size)]))
-    return jnp.stack(pieces)
+    return jnp.concatenate(pieces, 0)
 
 
 def exchange(blocks, axis):
@@ -53,7 +35,7 @@
 def per_device(tokens, expert_ids, gate_values, gate_up, down_weight, shared_gate_up, shared_down):
     experts, groups = lax.axis_size("expert"), lax.axis_size("group")
     me = lax.axis_index("expert")
-    count, width = tokens.shape
+    count, _ = tokens.shape
     columns = shared_gate_up.shape[0]
     units = shared_gate_up.shape[2]
 
@@ -71,8 +53,8 @@
     rows = jnp.dot(mine, tokens, preferred_element_type=jnp.float32).astype(jnp.bfloat16)
 
     own_columns = lax.dynamic_slice_in_dim(tokens, me * columns, columns, 1)
-    all_rows = gather_blocks(rows, "group").reshape(groups * CAP, width)
-    all_columns = gather_blocks(own_columns, "group").reshape(groups * count, columns)
+    all_rows = gather_blocks(rows, "group")
+    all_columns = gather_blocks(own_columns, "group")
 
     shared_gate, shared_up = gated(all_columns, shared_gate_up)
     partial = jnp.concatenate([shared_gate, shared_up], 1)
@@ -99,7 +81,8 @@
     shared = jnp.dot(shared_hidden, shared_down, preferred_element_type=jnp.float32).astype(jnp.bfloat16)
 
     arrived = exchange(shared.reshape(groups, count, columns), "group")
-    routed_arrived = exchange(jnp.swapaxes(routed, 0, 1).reshape(groups, experts * CAP, columns), "group")
+    routed_blocks = jnp.swapaxes(routed, 0, 1).reshape(groups, experts * CAP, columns)
+    routed_arrived = exchange(routed_blocks, "group")
     total = sum(a.astype(jnp.float32) for a in arrived)
     terms = sum(a.astype(jnp.float32) for a in routed_arrived)
     spread = jnp.where(selection, weight[:, None, :], 0.0).reshape(experts * CAP, count)
@@ -119,6 +102,5 @@
         P("group", "expert"),
     )
     out_specs = P(("dp", "group"), "expert")
-    return jax.shard_map(
-        per_device, mesh=mesh, in_specs=in_specs, out_specs=out_specs, check_vma=False
-    )
+
+    return jax.shard_map(per_device, mesh=mesh, in_specs=in_specs, out_specs=out_specs, check_vma=False)

time: 55.1 us -> 54.3 us (0.985)
  matrix products: 13.9 us -> 16 us
  other arithmetic: 5.07 us -> 3.52 us
  local copies, waits for them, and re-layouts: 2.51 us -> 1.17 us
    dot_general x2, matrix products: 12 us -> 14 us  [gated(): jnp.einsum('td,dgf->gtf', rows, weight, preferred_element_type=jnp.float32)]
    another operation x2 -> x0, other arithmetic: 1.55 us -> none  [gather_blocks(): return jnp.stack(pieces)]
    reshape x1 -> x0, local copies, waits for them, and re-layouts: 0.7 us -> none  [per_device(): all_rows = gather_blocks(rows, 'group').reshape(groups * CAP, width)]
    another operation x1 -> x0, local copies, waits for them, and re-layouts: 0.64 us -> none  [gather_blocks(): return jnp.stack(pieces)]
  transfers between devices with their start and end apart: 14 -> 14, of which waited for: 4 -> 4; matrix products, arithmetic and copies ran while one was open for 34% -> 33% of each run, Pallas kernels for 0% -> 0%
where the time goes in v2:
time: 54.3 us; the launch traced here: 54.1 us
  starting transfers between devices  22.3 us (41%)
  matrix products  16 us (29%)
  waiting for transfers between devices  10.9 us (20%)
  other arithmetic  3.52 us (6%)
  local copies, waits for them, and re-layouts  1.17 us (2%)
    dot_general x2, matrix products, gated(): jnp.einsum('td,dgf->gtf', rows, weight, preferred_element_type=jnp.float32)  14 us
    ppermute x6, starting transfers between devices, gather_blocks(): lax.ppermute(block, axis, [(i, (i - step) % size) for i in range(size)])  10.1 us
    ppermute x6, starting transfers between devices, exchange(): lax.ppermute(blocks[step], axis, [(i, (i + step) % size) for i in range(s...  9.1 us
    ppermute x6, waiting for transfers between devices, exchange(): lax.ppermute(blocks[step], axis, [(i, (i + step) % size) for i in range(s...  4.75 us
    ppermute x1, waiting for transfers between devices, per_device(): lax.ppermute(partial.astype(jnp.bfloat16), 'expert', [(0, 1), (1, 0)])  3.43 us
    ppermute x1, waiting for transfers between devices, per_device(): came = lax.ppermute(away, 'expert', [(0, 1), (1, 0)])  2.68 us
    ppermute x1, starting transfers between devices, per_device(): lax.ppermute(partial.astype(jnp.bfloat16), 'expert', [(0, 1), (1, 0)])  1.56 us
    ppermute x1, starting transfers between devices, per_device(): came = lax.ppermute(away, 'expert', [(0, 1), (1, 0)])  1.53 us
  transfers between devices with their start and end apart: 14, of which 4 were waited for; matrix products, arithmetic and copies ran while one was open for 33% of the time, Pallas kernels for 0%

profile of v2, /device:TPU:0, one launch (start us, length us, event | category | flops | bytes accessed | tf_op | source)
XLA Modules:
  0.0 54.1 jit_solution(17500007914517131234)
XLA Ops:
  0.0 0.7 %fusion.30 = pred[2,16]{1,0:T(4,128)(4,1)S(1)} fusion(s32[16,8]{0,1:T(8,128)} %param.8), kind=kLoop, calls=%fused_computation.50 | loop fusion | flops 480 | bytes 544 | tf_op jit(solution)/shard_map/reduce_or | solution.py:44
  0.8 0.1 iota_compare_fusion
  0.8 0.1 convert_reduce_fusion
  1.0 0.2 convolution_convert_fusion.1
  1.2 5.1 %collective-permute-start.7 = (bf16[2,7168]{1,0:T(2,128)(2,1)S(1)}, bf16[2,7168]{1,0:T(2,128)(2,1)S(1)}, u32[]{:S(2)}, u32[]{:S(2)}) collective-permute-start(bf16[2,7168]{1,0:T(2,128)(2,1)S(1)} %convolution_convert_fusion.1), channel_id=1, source_target_pairs={{0,3},{1,0},{2,1},{3,2},{4,7},{5,4},{6,5},{7,6},{8,11},{9,8},{10,9... | collective-permute-start | bytes 86024 | tf_op jit(solution)/shard_map/ppermute | solution.py:23
  6.3 0.0 collective-permute-start.8
  6.3 1.0 %collective-permute-start.9 = (bf16[2,7168]{1,0:T(2,128)(2,1)S(1)}, bf16[2,7168]{1,0:T(2,128)(2,1)S(1)}, u32[]{:S(2)}, u32[]{:S(2)}) collective-permute-start(bf16[2,7168]{1,0:T(2,128)(2,1)S(1)} %convolution_convert_fusion.1), channel_id=1, source_target_pairs={{0,1},{1,2},{2,3},{3,0},{4,5},{5,6},{6,7},{7,4},{8,9},{9,10},{10,1... | collective-permute-start | bytes 86024 | tf_op jit(solution)/shard_map/ppermute | solution.py:23
  7.3 0.7 %constant_dynamic-slice_fusion.2 = bf16[16,3584]{1,0:T(8,128)(2,1)} fusion(bf16[16,7168]{1,0:T(8,128)(2,1)S(1)} %copy-done, s32[]{:T(128)S(6)} %select_n.39), kind=kLoop, calls=%fused_computation.57 | loop fusion | bytes 229380 | tf_op jit(solution)/shard_map/dynamic_slice | solution.py:55
  8.0 2.8 %collective-permute-start = (bf16[16,3584]{1,0:T(8,128)(2,1)}, bf16[16,3584]{1,0:T(8,128)(2,1)}, u32[]{:S(2)}, u32[]{:S(2)}) collective-permute-start(bf16[16,3584]{1,0:T(8,128)(2,1)} %constant_dynamic-slice_fusion.2), channel_id=1, source_target_pairs={{0,3},{1,0},{2,1},{3,2},{4,7},{5,4},{6,5},{7,6},{8,11},{9,8},{10,9... | collective-permute-start | bytes 344072 | tf_op jit(solution)/shard_map/ppermute | solution.py:23
  10.8 1.1 %collective-permute-start.1 = (bf16[16,3584]{1,0:T(8,128)(2,1)}, bf16[16,3584]{1,0:T(8,128)(2,1)}, u32[]{:S(2)}, u32[]{:S(2)}) collective-permute-start(bf16[16,3584]{1,0:T(8,128)(2,1)} %constant_dynamic-slice_fusion.2), channel_id=1, source_target_pairs={{0,2},{1,3},{2,0},{3,1},{4,6},{5,7},{6,4},{7,5},{8,10},{9,11},{10,... | collective-permute-start | bytes 344072 | tf_op jit(solution)/shard_map/ppermute | solution.py:23
  11.9 0.7 %convert_element_type.70 = f32[16,8]{0,1:T(8,128)S(1)} convert(bf16[16,8]{0,1:T(8,128)(2,1)} %param.9) | non-fusion elementwise | flops 128 | bytes 768 | tf_op jit(solution)/shard_map/convert_element_type | solution.py:45
  12.6 0.7 %select_reduce_fusion = f32[2,16]{1,0:T(2,128)S(1)} fusion(f32[16,8]{0,1:T(8,128)S(1)} %convert_element_type.70, s32[16,8]{0,1:T(8,128)} %param.8), kind=kLoop, calls=%fused_computation.47 | loop fusion | flops 736 | bytes 1152 | tf_op jit(solution)/shard_map/reduce_sum | solution.py:45
  13.3 0.1 eq.47
  13.4 0.1 and_select_fusion
  13.5 0.0 collective-permute-done.7
  13.5 0.0 collective-permute-start.2
  13.5 0.0 collective-permute-done.8
  13.5 0.0 collective-permute-done.9
  13.5 0.0 slice-start.1
  13.5 9.1 %fusion.8 = f32[2,8,512]{2,1,0:T(8,128)S(1)} fusion(bf16[7168,2,512]{2,1,0:T(2,128)(2,1)} %bitcast.52, bf16[2,7168]{1,0:T(2,128)(2,1)S(1)} %collective-permute-done.9, bf16[2,7168]{1,0:T(2,128)(2,1)S(1)} %collective-permute-done.8, bf16[2,7168]{1,0:T(2,128)(2,1)S(1)} %collective-permute-done.7, bf16[2,7168]{1,0:T(2,128)(2,1)S(1)} %convolution_convert_fusion.1), kind=kOutput, calls=%fused_computation.9 | convolution fusion | flops 117899264 | bytes 14827520 | tf_op jit(solution)/shard_map/td,dgf->gtf/dot_general | solution.py:11
  22.7 1.1 %convolution_convert_fusion = bf16[8,7168]{1,0:T(8,128)(2,1)S(1)} fusion(bf16[1,512,7168]{2,1,0:T(8,128)(2,1)S(1)} %bitcast.54, f32[2,8,512]{2,1,0:T(8,128)S(1)} %fusion.8), kind=kOutput, calls=%fused_computation.2 | convolution fusion | flops 58802176 | bytes 7487488 | tf_op jit(solution)/shard_map/dot_general | solution.py:68
  23.7 1.5 %collective-permute-start.10 = (bf16[8,3584]{1,0:T(8,128)(2,1)S(1)}, bf16[8,3584]{1,0:T(8,128)(2,1)S(1)}, u32[]{:S(2)}, u32[]{:S(2)}) collective-permute-start(bf16[8,3584]{1,0:T(8,128)(2,1)S(1)} %dynamic-slice_bitcast_fusion), channel_id=1, source_target_pairs={{0,4},{4,0},{1,5},{5,1},{2,6},{6,2},{3,7},{7,3},{8,12},{12,8},{9,1... | collective-permute-start | bytes 172040 | tf_op jit(solution)/shard_map/ppermute | solution.py:73
  25.3 2.7 %collective-permute-done.10 = bf16[8,3584]{1,0:T(8,128)(2,1)S(1)} collective-permute-done((bf16[8,3584]{1,0:T(8,128)(2,1)S(1)}, bf16[8,3584]{1,0:T(8,128)(2,1)S(1)}, u32[]{:S(2)}, u32[]{:S(2)}) %collective-permute-start.10) | collective-permute-done | bytes 57376 | tf_op jit(solution)/shard_map/ppermute | solution.py:73
  28.0 0.2 maximum_bitcast_fusion.4
  28.2 0.1 fusion.42
  28.3 2.4 %collective-permute-start.11 = (bf16[4,3584]{1,0:T(4,128)(2,1)S(1)}, bf16[4,3584]{1,0:T(4,128)(2,1)S(1)}, u32[]{:S(2)}, u32[]{:S(2)}) collective-permute-start(bf16[4,3584]{1,0:T(4,128)(2,1)S(1)} %squeeze.46), channel_id=1, source_target_pairs={{0,1},{1,2},{2,3},{3,0},{4,5},{5,6},{6,7},{7,4},{8,9},{9,10},{10,1... | collective-permute-start | bytes 86024 | tf_op jit(solution)/shard_map/ppermute | solution.py:31
  30.7 2.1 %collective-permute-start.12 = (bf16[4,3584]{1,0:T(4,128)(2,1)S(1)}, bf16[4,3584]{1,0:T(4,128)(2,1)S(1)}, u32[]{:S(2)}, u32[]{:S(2)}) collective-permute-start(bf16[4,3584]{1,0:T(4,128)(2,1)S(1)} %squeeze.47), channel_id=1, source_target_pairs={{0,2},{1,3},{2,0},{3,1},{4,6},{5,7},{6,4},{7,5},{8,10},{9,11},{10,... | collective-permute-start | bytes 86024 | tf_op jit(solution)/shard_map/ppermute | solution.py:31
  32.8 0.1 reshape.57
  32.9 0.0 copy-start.1
  32.9 0.0 collective-permute-done
  32.9 0.4 collective-permute-start.13
  33.3 0.0 collective-permute-done.1
  33.3 0.0 collective-permute-done.2
  33.3 4.9 %fusion.5 = f32[2,64,512]{2,1,0:T(8,128)S(1)} fusion(bf16[3584,2,512]{2,1,0:T(2,128)(2,1)} %param.12, bf16[16,3584]{1,0:T(8,128)(2,1)} %collective-permute-done.2, bf16[16,3584]{1,0:T(8,128)(2,1)} %collective-permute-done.1, bf16[16,3584]{1,0:T(8,128)(2,1)} %collective-permute-done, bf16[16,3584]{1,0:T(8,128)(2,1)} %constant_dynamic-slice_fusion.2), kind=kOutput, calls=%fused_computation.8 | convolution fusion | flops 471597056 | bytes 8060928 | tf_op jit(solution)/shard_map/td,dgf->gtf/dot_general | solution.py:11
  38.3 1.6 %collective-permute-start.3 = (bf16[64,1024]{1,0:T(8,128)(2,1)S(1)}, bf16[64,1024]{1,0:T(8,128)(2,1)S(1)}, u32[]{:S(2)}, u32[]{:S(2)}) collective-permute-start(bf16[64,1024]{1,0:T(8,128)(2,1)S(1)} %fusion.17), channel_id=1, source_target_pairs={{0,4},{4,0},{1,5},{5,1},{2,6},{6,2},{3,7},{7,3},{8,12},{12,8},{9,1... | collective-permute-start | bytes 393224 | tf_op jit(solution)/shard_map/ppermute | solution.py:62
  39.9 0.0 collective-permute-done.11
  39.9 0.0 collective-permute-done.12
  39.9 0.0 collective-permute-done.13
  39.9 3.4 %collective-permute-done.3 = bf16[64,1024]{1,0:T(8,128)(2,1)S(1)} collective-permute-done((bf16[64,1024]{1,0:T(8,128)(2,1)S(1)}, bf16[64,1024]{1,0:T(8,128)(2,1)S(1)}, u32[]{:S(2)}, u32[]{:S(2)}) %collective-permute-start.3) | collective-permute-done | bytes 131104 | tf_op jit(solution)/shard_map/ppermute | solution.py:62
  43.4 0.7 %convolution_convert_fusion.2 = bf16[64,3584]{1,0:T(8,128)(2,1)S(1)} fusion(bf16[512,3584]{1,0:T(8,128)(2,1)S(1)} %copy-done.1, f32[64,1024]{1,0:T(8,128)S(1)} %convert_add_fusion), kind=kOutput, calls=%fused_computation.7 | convolution fusion | flops 235307008 | bytes 4390912 | tf_op jit(solution)/shard_map/dot_general | solution.py:81
  44.2 1.5 %collective-permute-start.4 = (bf16[16,3584]{1,0:T(8,128)(2,1)S(1)}, bf16[16,3584]{1,0:T(8,128)(2,1)S(1)}, u32[]{:S(2)}, u32[]{:S(2)}) collective-permute-start(bf16[16,3584]{1,0:T(8,128)(2,1)S(1)} %get-tuple-element.9), channel_id=1, source_target_pairs={{0,1},{1,2},{2,3},{3,0},{4,5},{5,6},{6,7},{7,4},{8,9},{9,10},{10,1... | collective-permute-start | bytes 344072 | tf_op jit(solution)/shard_map/ppermute | solution.py:31
  45.7 0.9 %collective-permute-start.5 = (bf16[16,3584]{1,0:T(8,128)(2,1)S(1)}, bf16[16,3584]{1,0:T(8,128)(2,1)S(1)}, u32[]{:S(2)}, u32[]{:S(2)}) collective-permute-start(bf16[16,3584]{1,0:T(8,128)(2,1)S(1)} %get-tuple-element.11), channel_id=1, source_target_pairs={{0,2},{1,3},{2,0},{3,1},{4,6},{5,7},{6,4},{7,5},{8,10},{9,11},{10,... | collective-permute-start | bytes 344072 | tf_op jit(solution)/shard_map/ppermute | solution.py:31
  46.6 1.8 %collective-permute-start.6 = (bf16[16,3584]{1,0:T(8,128)(2,1)S(1)}, bf16[16,3584]{1,0:T(8,128)(2,1)S(1)}, u32[]{:S(2)}, u32[]{:S(2)}) collective-permute-start(bf16[16,3584]{1,0:T(8,128)(2,1)S(1)} %get-tuple-element.10), channel_id=1, source_target_pairs={{0,3},{1,0},{2,1},{3,2},{4,7},{5,4},{6,5},{7,6},{8,11},{9,8},{10,9... | collective-permute-start | bytes 344072 | tf_op jit(solution)/shard_map/ppermute | solution.py:31
  48.4 0.1 slice_reduce_fusion.3
  48.5 2.4 %collective-permute-done.4 = bf16[16,3584]{1,0:T(8,128)(2,1)S(1)} collective-permute-done((bf16[16,3584]{1,0:T(8,128)(2,1)S(1)}, bf16[16,3584]{1,0:T(8,128)(2,1)S(1)}, u32[]{:S(2)}, u32[]{:S(2)}) %collective-permute-start.4) | collective-permute-done | bytes 114720 | tf_op jit(solution)/shard_map/ppermute | solution.py:31
  51.0 2.3 %collective-permute-done.5 = bf16[16,3584]{1,0:T(8,128)(2,1)S(1)} collective-permute-done((bf16[16,3584]{1,0:T(8,128)(2,1)S(1)}, bf16[16,3584]{1,0:T(8,128)(2,1)S(1)}, u32[]{:S(2)}, u32[]{:S(2)}) %collective-permute-start.5) | collective-permute-done | bytes 114720 | tf_op jit(solution)/shard_map/ppermute | solution.py:31
  53.3 0.0 collective-permute-done.6
  53.3 0.8 %add_convert_fusion = bf16[16,3584]{1,0:T(8,128)(2,1)} fusion(bf16[16,3584]{1,0:T(8,128)(2,1)S(1)} %collective-permute-done.6, bf16[16,3584]{1,0:T(8,128)(2,1)S(1)} %collective-permute-done.5, bf16[16,3584]{1,0:T(8,128)(2,1)S(1)} %collective-permute-done.4, bf16[64,3584]{1,0:T(8,128)(2,1)S(1)} %convolution_convert_fusion.2, f32[3584]{0:T(1024)S(1)} %get-tuple-element.6, ...), kind=kLoop, calls=%fused_computation.19 | loop fusion | flops 917504 | bytes 631040 | tf_op jit(solution)/shard_map/convert_element_type | solution.py:91
  (28 shorter events, 0.3 us)
Async XLA Ops:
  0.0 1.0 %copy-start = (bf16[16,7168]{1,0:T(8,128)(2,1)S(1)}, bf16[16,7168]{1,0:T(8,128)(2,1)}, u32[]{:S(2)}) copy-start(bf16[16,7168]{1,0:T(8,128)(2,1)} %param.7) | copy-start | bytes 688132
  1.2 12.3 %collective-permute-start.7 = (bf16[2,7168]{1,0:T(2,128)(2,1)S(1)}, bf16[2,7168]{1,0:T(2,128)(2,1)S(1)}, u32[]{:S(2)}, u32[]{:S(2)}) collective-permute-start(bf16[2,7168]{1,0:T(2,128)(2,1)S(1)} %convolution_convert_fusion.1), channel_id=1, source_target_pairs={{0,3},{1,0},{2,1},{3,2},{4,7},{5,4},{6,5},{7,6},{8,11},{9,8},{10,9... | collective-permute-start | bytes 86024 | tf_op jit(solution)/shard_map/ppermute | solution.py:23
  6.3 7.2 %collective-permute-start.8 = (bf16[2,7168]{1,0:T(2,128)(2,1)S(1)}, bf16[2,7168]{1,0:T(2,128)(2,1)S(1)}, u32[]{:S(2)}, u32[]{:S(2)}) collective-permute-start(bf16[2,7168]{1,0:T(2,128)(2,1)S(1)} %convolution_convert_fusion.1), channel_id=1, source_target_pairs={{0,2},{1,3},{2,0},{3,1},{4,6},{5,7},{6,4},{7,5},{8,10},{9,11},{10,... | collective-permute-start | bytes 86024 | tf_op jit(solution)/shard_map/ppermute | solution.py:23
  6.3 7.2 %collective-permute-start.9 = (bf16[2,7168]{1,0:T(2,128)(2,1)S(1)}, bf16[2,7168]{1,0:T(2,128)(2,1)S(1)}, u32[]{:S(2)}, u32[]{:S(2)}) collective-permute-start(bf16[2,7168]{1,0:T(2,128)(2,1)S(1)} %convolution_convert_fusion.1), channel_id=1, source_target_pairs={{0,1},{1,2},{2,3},{3,0},{4,5},{5,6},{6,7},{7,4},{8,9},{9,10},{10,1... | collective-permute-start | bytes 86024 | tf_op jit(solution)/shard_map/ppermute | solution.py:23
  7.3 15.4 %slice-start = ((s8[7340032]{0:T(1024)(128)(4,1)}), s8[3145728]{0:T(1024)(128)(4,1)S(1)}, s32[]{:S(2)}) async-start(s8[7340032]{0:T(1024)(128)(4,1)} %bitcast.53), calls=%async_computation | async-start | bytes 6291456
  8.0 24.9 %collective-permute-start = (bf16[16,3584]{1,0:T(8,128)(2,1)}, bf16[16,3584]{1,0:T(8,128)(2,1)}, u32[]{:S(2)}, u32[]{:S(2)}) collective-permute-start(bf16[16,3584]{1,0:T(8,128)(2,1)} %constant_dynamic-slice_fusion.2), channel_id=1, source_target_pairs={{0,3},{1,0},{2,1},{3,2},{4,7},{5,4},{6,5},{7,6},{8,11},{9,8},{10,9... | collective-permute-start | bytes 344072 | tf_op jit(solution)/shard_map/ppermute | solution.py:23
  10.8 22.6 %collective-permute-start.1 = (bf16[16,3584]{1,0:T(8,128)(2,1)}, bf16[16,3584]{1,0:T(8,128)(2,1)}, u32[]{:S(2)}, u32[]{:S(2)}) collective-permute-start(bf16[16,3584]{1,0:T(8,128)(2,1)} %constant_dynamic-slice_fusion.2), channel_id=1, source_target_pairs={{0,2},{1,3},{2,0},{3,1},{4,6},{5,7},{6,4},{7,5},{8,10},{9,11},{10,... | collective-permute-start | bytes 344072 | tf_op jit(solution)/shard_map/ppermute | solution.py:23
  13.5 19.9 %collective-permute-start.2 = (bf16[16,3584]{1,0:T(8,128)(2,1)}, bf16[16,3584]{1,0:T(8,128)(2,1)}, u32[]{:S(2)}, u32[]{:S(2)}) collective-permute-start(bf16[16,3584]{1,0:T(8,128)(2,1)} %constant_dynamic-slice_fusion.2), channel_id=1, source_target_pairs={{0,1},{1,2},{2,3},{3,0},{4,5},{5,6},{6,7},{7,4},{8,9},{9,10},{10,1... | collective-permute-start | bytes 344072 | tf_op jit(solution)/shard_map/ppermute | solution.py:23
  13.5 9.1 %slice-start.1 = ((s8[7340032]{0:T(1024)(128)(4,1)}), s8[4194304]{0:T(1024)(128)(4,1)S(1)}, s32[]{:S(2)}) async-start(s8[7340032]{0:T(1024)(128)(4,1)} %bitcast.53), calls=%async_computation.1 | async-start | bytes 8388608
  23.7 4.2 %collective-permute-start.10 = (bf16[8,3584]{1,0:T(8,128)(2,1)S(1)}, bf16[8,3584]{1,0:T(8,128)(2,1)S(1)}, u32[]{:S(2)}, u32[]{:S(2)}) collective-permute-start(bf16[8,3584]{1,0:T(8,128)(2,1)S(1)} %dynamic-slice_bitcast_fusion), channel_id=1, source_target_pairs={{0,4},{4,0},{1,5},{5,1},{2,6},{6,2},{3,7},{7,3},{8,12},{12,8},{9,1... | collective-permute-start | bytes 172040 | tf_op jit(solution)/shard_map/ppermute | solution.py:73
  28.3 11.6 %collective-permute-start.11 = (bf16[4,3584]{1,0:T(4,128)(2,1)S(1)}, bf16[4,3584]{1,0:T(4,128)(2,1)S(1)}, u32[]{:S(2)}, u32[]{:S(2)}) collective-permute-start(bf16[4,3584]{1,0:T(4,128)(2,1)S(1)} %squeeze.46), channel_id=1, source_target_pairs={{0,1},{1,2},{2,3},{3,0},{4,5},{5,6},{6,7},{7,4},{8,9},{9,10},{10,1... | collective-permute-start | bytes 86024 | tf_op jit(solution)/shard_map/ppermute | solution.py:31
  30.7 9.2 %collective-permute-start.12 = (bf16[4,3584]{1,0:T(4,128)(2,1)S(1)}, bf16[4,3584]{1,0:T(4,128)(2,1)S(1)}, u32[]{:S(2)}, u32[]{:S(2)}) collective-permute-start(bf16[4,3584]{1,0:T(4,128)(2,1)S(1)} %squeeze.47), channel_id=1, source_target_pairs={{0,2},{1,3},{2,0},{3,1},{4,6},{5,7},{6,4},{7,5},{8,10},{9,11},{10,... | collective-permute-start | bytes 86024 | tf_op jit(solution)/shard_map/ppermute | solution.py:31
  32.9 10.5 %copy-start.1 = (bf16[512,3584]{1,0:T(8,128)(2,1)S(1)}, bf16[512,3584]{1,0:T(8,128)(2,1)}, u32[]{:S(2)}) copy-start(bf16[512,3584]{1,0:T(8,128)(2,1)} %param.13) | copy-start | bytes 11010052
  32.9 7.0 %collective-permute-start.13 = (bf16[4,3584]{1,0:T(4,128)(2,1)S(1)}, bf16[4,3584]{1,0:T(4,128)(2,1)S(1)}, u32[]{:S(2)}, u32[]{:S(2)}) collective-permute-start(bf16[4,3584]{1,0:T(4,128)(2,1)S(1)} %squeeze.48), channel_id=1, source_target_pairs={{0,3},{1,0},{2,1},{3,2},{4,7},{5,4},{6,5},{7,6},{8,11},{9,8},{10,9... | collective-permute-start | bytes 86024 | tf_op jit(solution)/shard_map/ppermute | solution.py:31
  38.3 5.0 %collective-permute-start.3 = (bf16[64,1024]{1,0:T(8,128)(2,1)S(1)}, bf16[64,1024]{1,0:T(8,128)(2,1)S(1)}, u32[]{:S(2)}, u32[]{:S(2)}) collective-permute-start(bf16[64,1024]{1,0:T(8,128)(2,1)S(1)} %fusion.17), channel_id=1, source_target_pairs={{0,4},{4,0},{1,5},{5,1},{2,6},{6,2},{3,7},{7,3},{8,12},{12,8},{9,1... | collective-permute-start | bytes 393224 | tf_op jit(solution)/shard_map/ppermute | solution.py:62
  44.2 6.8 %collective-permute-start.4 = (bf16[16,3584]{1,0:T(8,128)(2,1)S(1)}, bf16[16,3584]{1,0:T(8,128)(2,1)S(1)}, u32[]{:S(2)}, u32[]{:S(2)}) collective-permute-start(bf16[16,3584]{1,0:T(8,128)(2,1)S(1)} %get-tuple-element.9), channel_id=1, source_target_pairs={{0,1},{1,2},{2,3},{3,0},{4,5},{5,6},{6,7},{7,4},{8,9},{9,10},{10,1... | collective-permute-start | bytes 344072 | tf_op jit(solution)/shard_map/ppermute | solution.py:31
  45.7 7.6 %collective-permute-start.5 = (bf16[16,3584]{1,0:T(8,128)(2,1)S(1)}, bf16[16,3584]{1,0:T(8,128)(2,1)S(1)}, u32[]{:S(2)}, u32[]{:S(2)}) collective-permute-start(bf16[16,3584]{1,0:T(8,128)(2,1)S(1)} %get-tuple-element.11), channel_id=1, source_target_pairs={{0,2},{1,3},{2,0},{3,1},{4,6},{5,7},{6,4},{7,5},{8,10},{9,11},{10,... | collective-permute-start | bytes 344072 | tf_op jit(solution)/shard_map/ppermute | solution.py:31
  46.6 6.7 %collective-permute-start.6 = (bf16[16,3584]{1,0:T(8,128)(2,1)S(1)}, bf16[16,3584]{1,0:T(8,128)(2,1)S(1)}, u32[]{:S(2)}, u32[]{:S(2)}) collective-permute-start(bf16[16,3584]{1,0:T(8,128)(2,1)S(1)} %get-tuple-element.10), channel_id=1, source_target_pairs={{0,3},{1,0},{2,1},{3,2},{4,7},{5,4},{6,5},{7,6},{8,11},{9,8},{10,9... | collective-permute-start | bytes 344072 | tf_op jit(solution)/shard_map/ppermute | solution.py:31

commit v3 on v2

--- a/solution.py
+++ b/solution.py
@@ -21,7 +21,7 @@
     pieces = [block]
     for step in range(1, size):
         pieces.append(lax.ppermute(block, axis, [(i, (i - step) % size) for i in range(size)]))
-    return jnp.concatenate(pieces, 0)
+    return pieces
 
 
 def exchange(blocks, axis):
@@ -35,7 +35,7 @@
 def per_device(tokens, expert_ids, gate_values, gate_up, down_weight, shared_gate_up, shared_down):
     experts, groups = lax.axis_size("expert"), lax.axis_size("group")
     me = lax.axis_index("expert")
-    count, _ = tokens.shape
+    count, width = tokens.shape
     columns = shared_gate_up.shape[0]
     units = shared_gate_up.shape[2]
 
@@ -53,8 +53,8 @@
     rows = jnp.dot(mine, tokens, preferred_element_type=jnp.float32).astype(jnp.bfloat16)
 
     own_columns = lax.dynamic_slice_in_dim(tokens, me * columns, columns, 1)
-    all_rows = gather_blocks(rows, "group")
-    all_columns = gather_blocks(own_columns, "group")
+    all_rows = jnp.stack(gather_blocks(rows, "group")).reshape(groups * CAP, width)
+    all_columns = jnp.concatenate(gather_blocks(own_columns, "group"), 0)
 
     shared_gate, shared_up = gated(all_columns, shared_gate_up)
     partial = jnp.concatenate([shared_gate, shared_up], 1)

time: 54.3 us -> 53.5 us (0.985)
  matrix products: 16 us -> 14.2 us
  starting transfers between devices: 22.3 us -> 23 us
  local copies, waits for them, and re-layouts: 1.17 us -> 1.85 us
    dot_general x2, matrix products: 14 us -> 12.2 us  [gated(): jnp.einsum('td,dgf->gtf', rows, weight, preferred_element_type=jnp.float32)]
    ppermute x6, starting transfers between devices: 9.1 us -> 9.89 us  [exchange(): lax.ppermute(blocks[step], axis, [(i, (i + step) % size) for i in range(s...]
    reshape x0 -> x1, local copies, waits for them, and re-layouts: none -> 0.68 us  [per_device(): jnp.stack(gather_blocks(rows, 'group')).reshape(groups * CAP, width)]
  transfers between devices with their start and end apart: 14 -> 14, of which waited for: 4 -> 4; matrix products, arithmetic and copies ran while one was open for 33% -> 32% of each run, Pallas kernels for 0% -> 0%
where the time goes in v3:
time: 53.5 us; the launch traced here: 53.3 us
  starting transfers between devices  23 us (43%)
  matrix products  14.2 us (27%)
  waiting for transfers between devices  10.4 us (19%)
  other arithmetic  3.72 us (7%)
  local copies, waits for them, and re-layouts  1.85 us (3%)
    dot_general x2, matrix products, gated(): jnp.einsum('td,dgf->gtf', rows, weight, preferred_element_type=jnp.float32)  12.2 us
    ppermute x6, starting transfers between devices, gather_blocks(): lax.ppermute(block, axis, [(i, (i - step) % size) for i in range(size)])  9.98 us
    ppermute x6, starting transfers between devices, exchange(): lax.ppermute(blocks[step], axis, [(i, (i + step) % size) for i in range(s...  9.89 us
    ppermute x6, waiting for transfers between devices, exchange(): lax.ppermute(blocks[step], axis, [(i, (i + step) % size) for i in range(s...  4.26 us
    ppermute x1, waiting for transfers between devices, per_device(): lax.ppermute(partial.astype(jnp.bfloat16), 'expert', [(0, 1), (1, 0)])  3.43 us
    ppermute x1, waiting for transfers between devices, per_device(): came = lax.ppermute(away, 'expert', [(0, 1), (1, 0)])  2.68 us
    ppermute x1, starting transfers between devices, per_device(): lax.ppermute(partial.astype(jnp.bfloat16), 'expert', [(0, 1), (1, 0)])  1.56 us
    ppermute x1, starting transfers between devices, per_device(): came = lax.ppermute(away, 'expert', [(0, 1), (1, 0)])  1.53 us
  transfers between devices with their start and end apart: 14, of which 4 were waited for; matrix products, arithmetic and copies ran while one was open for 32% of the time, Pallas kernels for 0%

profile of v3, /device:TPU:0, one launch (start us, length us, event | category | flops | bytes accessed | tf_op | source)
XLA Modules:
  0.0 53.3 jit_solution(18110998449796041848)
XLA Ops:
  0.0 0.7 %fusion.24 = pred[2,16]{1,0:T(4,128)(4,1)S(1)} fusion(s32[16,8]{0,1:T(8,128)} %param.8), kind=kLoop, calls=%fused_computation.44 | loop fusion | flops 480 | bytes 544 | tf_op jit(solution)/shard_map/reduce_or | solution.py:44
  0.8 0.1 iota_compare_fusion
  0.8 0.1 convert_reduce_fusion
  1.0 0.2 convolution_convert_fusion.1
  1.2 4.1 %collective-permute-start.8 = (bf16[2,7168]{1,0:T(2,128)(2,1)S(1)}, bf16[2,7168]{1,0:T(2,128)(2,1)S(1)}, u32[]{:S(2)}, u32[]{:S(2)}) collective-permute-start(bf16[2,7168]{1,0:T(2,128)(2,1)S(1)} %convolution_convert_fusion.1), channel_id=1, source_target_pairs={{0,2},{1,3},{2,0},{3,1},{4,6},{5,7},{6,4},{7,5},{8,10},{9,11},{10,... | collective-permute-start | bytes 86024 | tf_op jit(solution)/shard_map/ppermute | solution.py:23
  5.3 1.6 %collective-permute-start.9 = (bf16[2,7168]{1,0:T(2,128)(2,1)S(1)}, bf16[2,7168]{1,0:T(2,128)(2,1)S(1)}, u32[]{:S(2)}, u32[]{:S(2)}) collective-permute-start(bf16[2,7168]{1,0:T(2,128)(2,1)S(1)} %convolution_convert_fusion.1), channel_id=1, source_target_pairs={{0,1},{1,2},{2,3},{3,0},{4,5},{5,6},{6,7},{7,4},{8,9},{9,10},{10,1... | collective-permute-start | bytes 86024 | tf_op jit(solution)/shard_map/ppermute | solution.py:23
  6.9 2.2 %collective-permute-start.7 = (bf16[2,7168]{1,0:T(2,128)(2,1)S(1)}, bf16[2,7168]{1,0:T(2,128)(2,1)S(1)}, u32[]{:S(2)}, u32[]{:S(2)}) collective-permute-start(bf16[2,7168]{1,0:T(2,128)(2,1)S(1)} %convolution_convert_fusion.1), channel_id=1, source_target_pairs={{0,3},{1,0},{2,1},{3,2},{4,7},{5,4},{6,5},{7,6},{8,11},{9,8},{10,9... | collective-permute-start | bytes 86024 | tf_op jit(solution)/shard_map/ppermute | solution.py:23
  9.1 0.7 %constant_dynamic-slice_fusion.2 = bf16[16,3584]{1,0:T(8,128)(2,1)} fusion(bf16[16,7168]{1,0:T(8,128)(2,1)S(1)} %copy-done, s32[]{:T(128)S(6)} %select_n.39), kind=kLoop, calls=%fused_computation.51 | loop fusion | bytes 229380 | tf_op jit(solution)/shard_map/dynamic_slice | solution.py:55
  9.8 0.0 collective-permute-start
  9.8 1.2 %collective-permute-start.1 = (bf16[16,3584]{1,0:T(8,128)(2,1)}, bf16[16,3584]{1,0:T(8,128)(2,1)}, u32[]{:S(2)}, u32[]{:S(2)}) collective-permute-start(bf16[16,3584]{1,0:T(8,128)(2,1)} %constant_dynamic-slice_fusion.2), channel_id=1, source_target_pairs={{0,2},{1,3},{2,0},{3,1},{4,6},{5,7},{6,4},{7,5},{8,10},{9,11},{10,... | collective-permute-start | bytes 344072 | tf_op jit(solution)/shard_map/ppermute | solution.py:23
  11.0 0.7 %convert_element_type.70 = f32[16,8]{0,1:T(8,128)S(1)} convert(bf16[16,8]{0,1:T(8,128)(2,1)} %param.9) | non-fusion elementwise | flops 128 | bytes 768 | tf_op jit(solution)/shard_map/convert_element_type | solution.py:45
  11.7 0.7 %select_reduce_fusion = f32[2,16]{1,0:T(2,128)S(1)} fusion(f32[16,8]{0,1:T(8,128)S(1)} %convert_element_type.70, s32[16,8]{0,1:T(8,128)} %param.8), kind=kLoop, calls=%fused_computation.41 | loop fusion | flops 736 | bytes 1152 | tf_op jit(solution)/shard_map/reduce_sum | solution.py:45
  12.4 0.1 eq.47
  12.5 0.1 and_select_fusion
  12.6 0.0 collective-permute-done.8
  12.6 0.8 %collective-permute-start.2 = (bf16[16,3584]{1,0:T(8,128)(2,1)}, bf16[16,3584]{1,0:T(8,128)(2,1)}, u32[]{:S(2)}, u32[]{:S(2)}) collective-permute-start(bf16[16,3584]{1,0:T(8,128)(2,1)} %constant_dynamic-slice_fusion.2), channel_id=1, source_target_pairs={{0,1},{1,2},{2,3},{3,0},{4,5},{5,6},{6,7},{7,4},{8,9},{9,10},{10,1... | collective-permute-start | bytes 344072 | tf_op jit(solution)/shard_map/ppermute | solution.py:23
  13.4 0.0 collective-permute-done.9
  13.4 0.0 collective-permute-done.7
  13.4 0.2 pad_maximum_fusion.1
  13.6 0.0 slice-start
  13.6 0.7 %reshape.63 = bf16[8,7168,1]{1,0,2:T(8,128)(2,1)} reshape(bf16[4,2,7168]{2,1,0:T(2,128)(2,1)S(1)} %pad_maximum_fusion.1) | data formatting | bytes 229376 | tf_op jit(solution)/shard_map/reshape | solution.py:56
  14.3 7.5 %fusion.8 = f32[2,8,512]{2,1,0:T(8,128)S(1)} fusion(bf16[8,7168,1]{1,0,2:T(8,128)(2,1)} %reshape.63, bf16[7168,2,512]{2,1,0:T(2,128)(2,1)} %bitcast.54), kind=kOutput, calls=%fused_computation.9 | convolution fusion | flops 117440512 | bytes 14827520 | tf_op jit(solution)/shard_map/td,dgf->gtf/dot_general | solution.py:11
  21.8 1.1 %convolution_convert_fusion = bf16[8,7168]{1,0:T(8,128)(2,1)S(1)} fusion(bf16[1,512,7168]{2,1,0:T(8,128)(2,1)S(1)} %bitcast.56, f32[2,8,512]{2,1,0:T(8,128)S(1)} %fusion.8), kind=kOutput, calls=%fused_computation.2 | convolution fusion | flops 58802176 | bytes 7487488 | tf_op jit(solution)/shard_map/dot_general | solution.py:68
  22.9 1.5 %collective-permute-start.10 = (bf16[8,3584]{1,0:T(8,128)(2,1)S(1)}, bf16[8,3584]{1,0:T(8,128)(2,1)S(1)}, u32[]{:S(2)}, u32[]{:S(2)}) collective-permute-start(bf16[8,3584]{1,0:T(8,128)(2,1)S(1)} %dynamic-slice_bitcast_fusion), channel_id=1, source_target_pairs={{0,4},{4,0},{1,5},{5,1},{2,6},{6,2},{3,7},{7,3},{8,12},{12,8},{9,1... | collective-permute-start | bytes 172040 | tf_op jit(solution)/shard_map/ppermute | solution.py:73
  24.4 2.7 %collective-permute-done.10 = bf16[8,3584]{1,0:T(8,128)(2,1)S(1)} collective-permute-done((bf16[8,3584]{1,0:T(8,128)(2,1)S(1)}, bf16[8,3584]{1,0:T(8,128)(2,1)S(1)}, u32[]{:S(2)}, u32[]{:S(2)}) %collective-permute-start.10) | collective-permute-done | bytes 57376 | tf_op jit(solution)/shard_map/ppermute | solution.py:73
  27.2 0.2 maximum_bitcast_fusion.2
  27.3 0.1 fusion.35
  27.5 1.5 %collective-permute-start.11 = (bf16[4,3584]{1,0:T(4,128)(2,1)S(1)}, bf16[4,3584]{1,0:T(4,128)(2,1)S(1)}, u32[]{:S(2)}, u32[]{:S(2)}) collective-permute-start(bf16[4,3584]{1,0:T(4,128)(2,1)S(1)} %squeeze.46), channel_id=1, source_target_pairs={{0,1},{1,2},{2,3},{3,0},{4,5},{5,6},{6,7},{7,4},{8,9},{9,10},{10,1... | collective-permute-start | bytes 86024 | tf_op jit(solution)/shard_map/ppermute | solution.py:31
  29.0 2.2 %collective-permute-start.12 = (bf16[4,3584]{1,0:T(4,128)(2,1)S(1)}, bf16[4,3584]{1,0:T(4,128)(2,1)S(1)}, u32[]{:S(2)}, u32[]{:S(2)}) collective-permute-start(bf16[4,3584]{1,0:T(4,128)(2,1)S(1)} %squeeze.47), channel_id=1, source_target_pairs={{0,2},{1,3},{2,0},{3,1},{4,6},{5,7},{6,4},{7,5},{8,10},{9,11},{10,... | collective-permute-start | bytes 86024 | tf_op jit(solution)/shard_map/ppermute | solution.py:31
  31.2 0.1 reshape.61
  31.3 0.0 copy-start.1
  31.3 0.0 collective-permute-done
  31.3 2.3 %collective-permute-start.13 = (bf16[4,3584]{1,0:T(4,128)(2,1)S(1)}, bf16[4,3584]{1,0:T(4,128)(2,1)S(1)}, u32[]{:S(2)}, u32[]{:S(2)}) collective-permute-start(bf16[4,3584]{1,0:T(4,128)(2,1)S(1)} %squeeze.48), channel_id=1, source_target_pairs={{0,3},{1,0},{2,1},{3,2},{4,7},{5,4},{6,5},{7,6},{8,11},{9,8},{10,9... | collective-permute-start | bytes 86024 | tf_op jit(solution)/shard_map/ppermute | solution.py:31
  33.6 0.0 collective-permute-done.1
  33.6 4.7 %fusion.5 = f32[2,64,512]{2,1,0:T(8,128)S(1)} fusion(bf16[3584,2,512]{2,1,0:T(2,128)(2,1)} %param.12, bf16[16,3584]{1,0:T(8,128)(2,1)} %collective-permute-done.2, bf16[16,3584]{1,0:T(8,128)(2,1)} %collective-permute-done.1, bf16[16,3584]{1,0:T(8,128)(2,1)} %collective-permute-done, bf16[16,3584]{1,0:T(8,128)(2,1)} %constant_dynamic-slice_fusion.2), kind=kOutput, calls=%fused_computation.8 | convolution fusion | flops 471597056 | bytes 8060928 | tf_op jit(solution)/shard_map/td,dgf->gtf/dot_general | solution.py:11
  38.4 1.6 %collective-permute-start.3 = (bf16[64,1024]{1,0:T(8,128)(2,1)S(1)}, bf16[64,1024]{1,0:T(8,128)(2,1)S(1)}, u32[]{:S(2)}, u32[]{:S(2)}) collective-permute-start(bf16[64,1024]{1,0:T(8,128)(2,1)S(1)} %fusion.17), channel_id=1, source_target_pairs={{0,4},{4,0},{1,5},{5,1},{2,6},{6,2},{3,7},{7,3},{8,12},{12,8},{9,1... | collective-permute-start | bytes 393224 | tf_op jit(solution)/shard_map/ppermute | solution.py:62
  39.9 0.0 collective-permute-done.12
  39.9 0.0 collective-permute-done.13
  40.0 3.4 %collective-permute-done.3 = bf16[64,1024]{1,0:T(8,128)(2,1)S(1)} collective-permute-done((bf16[64,1024]{1,0:T(8,128)(2,1)S(1)}, bf16[64,1024]{1,0:T(8,128)(2,1)S(1)}, u32[]{:S(2)}, u32[]{:S(2)}) %collective-permute-start.3) | collective-permute-done | bytes 131104 | tf_op jit(solution)/shard_map/ppermute | solution.py:62
  43.5 0.7 %convolution_convert_fusion.2 = bf16[64,3584]{1,0:T(8,128)(2,1)S(1)} fusion(bf16[512,3584]{1,0:T(8,128)(2,1)S(1)} %copy-done.1, f32[64,1024]{1,0:T(8,128)S(1)} %convert_add_fusion), kind=kOutput, calls=%fused_computation.7 | convolution fusion | flops 235307008 | bytes 4390912 | tf_op jit(solution)/shard_map/dot_general | solution.py:81
  44.2 0.1 collective-permute-start.4
  44.3 0.7 %collective-permute-start.5 = (bf16[16,3584]{1,0:T(8,128)(2,1)S(1)}, bf16[16,3584]{1,0:T(8,128)(2,1)S(1)}, u32[]{:S(2)}, u32[]{:S(2)}) collective-permute-start(bf16[16,3584]{1,0:T(8,128)(2,1)S(1)} %get-tuple-element.11), channel_id=1, source_target_pairs={{0,2},{1,3},{2,0},{3,1},{4,6},{5,7},{6,4},{7,5},{8,10},{9,11},{10,... | collective-permute-start | bytes 344072 | tf_op jit(solution)/shard_map/ppermute | solution.py:31
  45.0 3.1 %collective-permute-start.6 = (bf16[16,3584]{1,0:T(8,128)(2,1)S(1)}, bf16[16,3584]{1,0:T(8,128)(2,1)S(1)}, u32[]{:S(2)}, u32[]{:S(2)}) collective-permute-start(bf16[16,3584]{1,0:T(8,128)(2,1)S(1)} %get-tuple-element.10), channel_id=1, source_target_pairs={{0,3},{1,0},{2,1},{3,2},{4,7},{5,4},{6,5},{7,6},{8,11},{9,8},{10,9... | collective-permute-start | bytes 344072 | tf_op jit(solution)/shard_map/ppermute | solution.py:31
  48.1 0.1 slice_reduce_fusion.3
  48.3 2.8 %collective-permute-done.4 = bf16[16,3584]{1,0:T(8,128)(2,1)S(1)} collective-permute-done((bf16[16,3584]{1,0:T(8,128)(2,1)S(1)}, bf16[16,3584]{1,0:T(8,128)(2,1)S(1)}, u32[]{:S(2)}, u32[]{:S(2)}) %collective-permute-start.4) | collective-permute-done | bytes 114720 | tf_op jit(solution)/shard_map/ppermute | solution.py:31
  51.1 1.5 %collective-permute-done.5 = bf16[16,3584]{1,0:T(8,128)(2,1)S(1)} collective-permute-done((bf16[16,3584]{1,0:T(8,128)(2,1)S(1)}, bf16[16,3584]{1,0:T(8,128)(2,1)S(1)}, u32[]{:S(2)}, u32[]{:S(2)}) %collective-permute-start.5) | collective-permute-done | bytes 114720 | tf_op jit(solution)/shard_map/ppermute | solution.py:31
  52.5 0.0 collective-permute-done.6
  52.5 0.8 %add_convert_fusion = bf16[16,3584]{1,0:T(8,128)(2,1)} fusion(bf16[16,3584]{1,0:T(8,128)(2,1)S(1)} %collective-permute-done.6, bf16[16,3584]{1,0:T(8,128)(2,1)S(1)} %collective-permute-done.5, bf16[16,3584]{1,0:T(8,128)(2,1)S(1)} %collective-permute-done.4, bf16[64,3584]{1,0:T(8,128)(2,1)S(1)} %convolution_convert_fusion.2, f32[3584]{0:T(1024)S(1)} %get-tuple-element.6, ...), kind=kLoop, calls=%fused_computation.19 | loop fusion | flops 917504 | bytes 631040 | tf_op jit(solution)/shard_map/convert_element_type | solution.py:91
  (30 shorter events, 0.3 us)
Async XLA Ops:
  0.0 1.0 %copy-start = (bf16[16,7168]{1,0:T(8,128)(2,1)S(1)}, bf16[16,7168]{1,0:T(8,128)(2,1)}, u32[]{:S(2)}) copy-start(bf16[16,7168]{1,0:T(8,128)(2,1)} %param.7) | copy-start | bytes 688132
  1.2 11.4 %collective-permute-start.8 = (bf16[2,7168]{1,0:T(2,128)(2,1)S(1)}, bf16[2,7168]{1,0:T(2,128)(2,1)S(1)}, u32[]{:S(2)}, u32[]{:S(2)}) collective-permute-start(bf16[2,7168]{1,0:T(2,128)(2,1)S(1)} %convolution_convert_fusion.1), channel_id=1, source_target_pairs={{0,2},{1,3},{2,0},{3,1},{4,6},{5,7},{6,4},{7,5},{8,10},{9,11},{10,... | collective-permute-start | bytes 86024 | tf_op jit(solution)/shard_map/ppermute | solution.py:23
  5.3 8.1 %collective-permute-start.9 = (bf16[2,7168]{1,0:T(2,128)(2,1)S(1)}, bf16[2,7168]{1,0:T(2,128)(2,1)S(1)}, u32[]{:S(2)}, u32[]{:S(2)}) collective-permute-start(bf16[2,7168]{1,0:T(2,128)(2,1)S(1)} %convolution_convert_fusion.1), channel_id=1, source_target_pairs={{0,1},{1,2},{2,3},{3,0},{4,5},{5,6},{6,7},{7,4},{8,9},{9,10},{10,1... | collective-permute-start | bytes 86024 | tf_op jit(solution)/shard_map/ppermute | solution.py:23
  6.9 6.5 %collective-permute-start.7 = (bf16[2,7168]{1,0:T(2,128)(2,1)S(1)}, bf16[2,7168]{1,0:T(2,128)(2,1)S(1)}, u32[]{:S(2)}, u32[]{:S(2)}) collective-permute-start(bf16[2,7168]{1,0:T(2,128)(2,1)S(1)} %convolution_convert_fusion.1), channel_id=1, source_target_pairs={{0,3},{1,0},{2,1},{3,2},{4,7},{5,4},{6,5},{7,6},{8,11},{9,8},{10,9... | collective-permute-start | bytes 86024 | tf_op jit(solution)/shard_map/ppermute | solution.py:23
  9.8 21.5 %collective-permute-start = (bf16[16,3584]{1,0:T(8,128)(2,1)}, bf16[16,3584]{1,0:T(8,128)(2,1)}, u32[]{:S(2)}, u32[]{:S(2)}) collective-permute-start(bf16[16,3584]{1,0:T(8,128)(2,1)} %constant_dynamic-slice_fusion.2), channel_id=1, source_target_pairs={{0,3},{1,0},{2,1},{3,2},{4,7},{5,4},{6,5},{7,6},{8,11},{9,8},{10,9... | collective-permute-start | bytes 344072 | tf_op jit(solution)/shard_map/ppermute | solution.py:23
  9.8 23.8 %collective-permute-start.1 = (bf16[16,3584]{1,0:T(8,128)(2,1)}, bf16[16,3584]{1,0:T(8,128)(2,1)}, u32[]{:S(2)}, u32[]{:S(2)}) collective-permute-start(bf16[16,3584]{1,0:T(8,128)(2,1)} %constant_dynamic-slice_fusion.2), channel_id=1, source_target_pairs={{0,2},{1,3},{2,0},{3,1},{4,6},{5,7},{6,4},{7,5},{8,10},{9,11},{10,... | collective-permute-start | bytes 344072 | tf_op jit(solution)/shard_map/ppermute | solution.py:23
  12.6 21.0 %collective-permute-start.2 = (bf16[16,3584]{1,0:T(8,128)(2,1)}, bf16[16,3584]{1,0:T(8,128)(2,1)}, u32[]{:S(2)}, u32[]{:S(2)}) collective-permute-start(bf16[16,3584]{1,0:T(8,128)(2,1)} %constant_dynamic-slice_fusion.2), channel_id=1, source_target_pairs={{0,1},{1,2},{2,3},{3,0},{4,5},{5,6},{6,7},{7,4},{8,9},{9,10},{10,1... | collective-permute-start | bytes 344072 | tf_op jit(solution)/shard_map/ppermute | solution.py:23
  13.6 8.2 %slice-start = ((s8[7340032]{0:T(1024)(128)(4,1)}), s8[3145728]{0:T(1024)(128)(4,1)S(1)}, s32[]{:S(2)}) async-start(s8[7340032]{0:T(1024)(128)(4,1)} %bitcast.55), calls=%async_computation | async-start | bytes 6291456
  14.3 7.5 %slice-start.1 = ((s8[7340032]{0:T(1024)(128)(4,1)}), s8[4194304]{0:T(1024)(128)(4,1)S(1)}, s32[]{:S(2)}) async-start(s8[7340032]{0:T(1024)(128)(4,1)} %bitcast.55), calls=%async_computation.1 | async-start | bytes 8388608
  22.9 4.2 %collective-permute-start.10 = (bf16[8,3584]{1,0:T(8,128)(2,1)S(1)}, bf16[8,3584]{1,0:T(8,128)(2,1)S(1)}, u32[]{:S(2)}, u32[]{:S(2)}) collective-permute-start(bf16[8,3584]{1,0:T(8,128)(2,1)S(1)} %dynamic-slice_bitcast_fusion), channel_id=1, source_target_pairs={{0,4},{4,0},{1,5},{5,1},{2,6},{6,2},{3,7},{7,3},{8,12},{12,8},{9,1... | collective-permute-start | bytes 172040 | tf_op jit(solution)/shard_map/ppermute | solution.py:73
  27.5 12.5 %collective-permute-start.11 = (bf16[4,3584]{1,0:T(4,128)(2,1)S(1)}, bf16[4,3584]{1,0:T(4,128)(2,1)S(1)}, u32[]{:S(2)}, u32[]{:S(2)}) collective-permute-start(bf16[4,3584]{1,0:T(4,128)(2,1)S(1)} %squeeze.46), channel_id=1, source_target_pairs={{0,1},{1,2},{2,3},{3,0},{4,5},{5,6},{6,7},{7,4},{8,9},{9,10},{10,1... | collective-permute-start | bytes 86024 | tf_op jit(solution)/shard_map/ppermute | solution.py:31
  29.0 11.0 %collective-permute-start.12 = (bf16[4,3584]{1,0:T(4,128)(2,1)S(1)}, bf16[4,3584]{1,0:T(4,128)(2,1)S(1)}, u32[]{:S(2)}, u32[]{:S(2)}) collective-permute-start(bf16[4,3584]{1,0:T(4,128)(2,1)S(1)} %squeeze.47), channel_id=1, source_target_pairs={{0,2},{1,3},{2,0},{3,1},{4,6},{5,7},{6,4},{7,5},{8,10},{9,11},{10,... | collective-permute-start | bytes 86024 | tf_op jit(solution)/shard_map/ppermute | solution.py:31
  31.3 12.2 %copy-start.1 = (bf16[512,3584]{1,0:T(8,128)(2,1)S(1)}, bf16[512,3584]{1,0:T(8,128)(2,1)}, u32[]{:S(2)}) copy-start(bf16[512,3584]{1,0:T(8,128)(2,1)} %param.13) | copy-start | bytes 11010052
  31.3 8.7 %collective-permute-start.13 = (bf16[4,3584]{1,0:T(4,128)(2,1)S(1)}, bf16[4,3584]{1,0:T(4,128)(2,1)S(1)}, u32[]{:S(2)}, u32[]{:S(2)}) collective-permute-start(bf16[4,3584]{1,0:T(4,128)(2,1)S(1)} %squeeze.48), channel_id=1, source_target_pairs={{0,3},{1,0},{2,1},{3,2},{4,7},{5,4},{6,5},{7,6},{8,11},{9,8},{10,9... | collective-permute-start | bytes 86024 | tf_op jit(solution)/shard_map/ppermute | solution.py:31
  38.4 5.0 %collective-permute-start.3 = (bf16[64,1024]{1,0:T(8,128)(2,1)S(1)}, bf16[64,1024]{1,0:T(8,128)(2,1)S(1)}, u32[]{:S(2)}, u32[]{:S(2)}) collective-permute-start(bf16[64,1024]{1,0:T(8,128)(2,1)S(1)} %fusion.17), channel_id=1, source_target_pairs={{0,4},{4,0},{1,5},{5,1},{2,6},{6,2},{3,7},{7,3},{8,12},{12,8},{9,1... | collective-permute-start | bytes 393224 | tf_op jit(solution)/shard_map/ppermute | solution.py:62
  44.2 6.8 %collective-permute-start.4 = (bf16[16,3584]{1,0:T(8,128)(2,1)S(1)}, bf16[16,3584]{1,0:T(8,128)(2,1)S(1)}, u32[]{:S(2)}, u32[]{:S(2)}) collective-permute-start(bf16[16,3584]{1,0:T(8,128)(2,1)S(1)} %get-tuple-element.9), channel_id=1, source_target_pairs={{0,1},{1,2},{2,3},{3,0},{4,5},{5,6},{6,7},{7,4},{8,9},{9,10},{10,1... | collective-permute-start | bytes 344072 | tf_op jit(solution)/shard_map/ppermute | solution.py:31
  44.3 8.2 %collective-permute-start.5 = (bf16[16,3584]{1,0:T(8,128)(2,1)S(1)}, bf16[16,3584]{1,0:T(8,128)(2,1)S(1)}, u32[]{:S(2)}, u32[]{:S(2)}) collective-permute-start(bf16[16,3584]{1,0:T(8,128)(2,1)S(1)} %get-tuple-element.11), channel_id=1, source_target_pairs={{0,2},{1,3},{2,0},{3,1},{4,6},{5,7},{6,4},{7,5},{8,10},{9,11},{10,... | collective-permute-start | bytes 344072 | tf_op jit(solution)/shard_map/ppermute | solution.py:31
  45.0 7.5 %collective-permute-start.6 = (bf16[16,3584]{1,0:T(8,128)(2,1)S(1)}, bf16[16,3584]{1,0:T(8,128)(2,1)S(1)}, u32[]{:S(2)}, u32[]{:S(2)}) collective-permute-start(bf16[16,3584]{1,0:T(8,128)(2,1)S(1)} %get-tuple-element.10), channel_id=1, source_target_pairs={{0,3},{1,0},{2,1},{3,2},{4,7},{5,4},{6,5},{7,6},{8,11},{9,8},{10,9... | collective-permute-start | bytes 344072 | tf_op jit(solution)/shard_map/ppermute | solution.py:31
